TPU v7x, 128 devices: a whole 4x4x4 slice. The times are simulated.
128 devices in a mesh: chan: 16 (over z, x), mode: 8 (over y, core).
Axes of the slice: x: 4, y: 4, z: 4, core: 2. Of those that a mesh axis runs over, the one named last changes fastest.
Arguments:
- weight: bfloat16 [512, 2, 32, 32, 256], P('chan', None, 'mode'), may hold values from -0.59765625 to 0.59765625
- gradient: bfloat16 [512, 2, 32, 32, 256], P('chan', None, 'mode'), may hold values from -6 to 6
- first_moment: float32 [128, 2, 16, 16, 128], P('chan', None, None, 'mode'), may hold values from -2 to 2
- second_moment: float32 [128, 2, 16, 16, 128], P('chan', None, None, 'mode'), may hold values from 0.0005 to 0.02
- u_in: float32 [512, 128], P('chan'), may hold values from -0.25 to 0.25
- u_out: bfloat16 [256, 128], replicated, may hold values from -0.375 to 0.375
- u_modes_a: float32 [32, 16], replicated, may hold values from -1 to 1
- u_modes_b: float32 [32, 16], replicated, may hold values from -1 to 1
Outputs:
- new_weight: bfloat16 [512, 2, 32, 32, 256], P('chan', None, 'mode')
- new_first: float32 [128, 2, 16, 16, 128], P('chan', None, None, 'mode')
- new_second: float32 [128, 2, 16, 16, 128], P('chan', None, None, 'mode')
All inputs are finite; a program needn't handle non-finite values.
Results may differ from a plain program's by a relative error of at most 0.004.
Values sent between devices are 32-bit elements; how exact they have to be, the bound alone decides.
No kernel may reach another device: no remote copies, remote signals or barrier semaphores. Data moves between devices by JAX's collectives and lax.ppermute only.
A program may use at most 128 MiB of HBM per device.

v0:
```python
import jax
import jax.numpy as jnp
from jax import lax
from jax.sharding import PartitionSpec as P

STEP = 4


HIGH = lax.Precision.HIGHEST
beta_one = 0.9
beta_two = 0.999
step_rate = 0.5


def shards(weight, gradient, first_moment, second_moment, u_in, u_out, u_modes_a, u_modes_b):
    local_in, parts, local_a, modes_b, out_ch = gradient.shape
    rank_out = u_out.shape[1]
    rank_in = u_in.shape[1]
    reduced = jnp.dot(gradient.reshape(-1, out_ch), u_out, preferred_element_type=jnp.float32)
    reduced = reduced.reshape(local_in, parts, local_a, modes_b, rank_out)
    narrowed = jnp.einsum("ipabo,bs->ipaso", reduced, u_modes_b, precision=HIGH)
    local_rows = lax.dynamic_slice_in_dim(u_modes_a, lax.axis_index("mode") * local_a, local_a, 0)
    owned_rows = rank_in // lax.axis_size("chan")
    partial_sum = jnp.einsum("ipaso,ar->iprso", narrowed, local_rows, precision=HIGH)
    mixed = lax.psum_scatter(partial_sum, "mode", scatter_dimension=3, tiled=True)
    summed = lax.psum(jnp.einsum("ik,iprso->kprso", u_in, mixed, precision=HIGH), "chan")
    core = lax.dynamic_slice_in_dim(summed, lax.axis_index("chan") * owned_rows, owned_rows, 0)
    new_first = beta_one * first_moment + (1.0 - beta_one) * core
    new_second = beta_two * second_moment + (1.0 - beta_two) * core * core
    direction = (
        new_first / (1.0 - beta_one**STEP) / (jnp.sqrt(new_second / (1.0 - beta_two**STEP)) + 1e-08)
    )
    spread = jnp.einsum(
        "ik,kprso->iprso",
        u_in,
        lax.all_gather(direction, "chan", axis=0, tiled=True),
        precision=HIGH,
    )
    full_ranks = lax.all_gather(spread, "mode", axis=3, tiled=True)
    wide = jnp.einsum("iprso,ar->ipaso", full_ranks, local_rows, precision=HIGH)
    expanded = jnp.einsum("ipaso,bs->ipabo", wide, u_modes_b, precision=HIGH).astype(jnp.bfloat16)
    update = jnp.dot(expanded.reshape(-1, rank_out), u_out.T, preferred_element_type=jnp.float32)
    update = update.reshape(weight.shape)
    new_weight = (weight.astype(jnp.float32) - step_rate * update).astype(jnp.bfloat16)
    return (new_weight, new_first, new_second)


def solution(mesh):
    in_specs = (
        P("chan", None, "mode", None, None),
        P("chan", None, "mode", None, None),
        P("chan", None, None, "mode", None),
        P("chan", None, None, "mode", None),
        P("chan", None),
        P(),
        P(),
        P(),
    )
    out_specs = (
        P("chan", None, "mode", None, None),
        P("chan", None, None, "mode", None),
        P("chan", None, None, "mode", None),
    )
    return jax.shard_map(shards, mesh=mesh, in_specs=in_specs, out_specs=out_specs, check_vma=False)
```

profile of v0, /device:TPU:1, one launch (start us, length us, event | category | flops | bytes accessed | tf_op | source)
XLA Modules:
  0.0 387.8 jit_solution(8471863617202038372)
XLA Ops:
  7.2 0.0 copy-start
  7.2 0.0 all-reduce.6.cloned.1.call-start
  7.2 0.8 copy-done
  8.0 3.4 fusion.20
  11.5 0.0 copy-start.5
  11.5 2.3 convolution_bitcast_fusion.1
  13.8 7.5 %convolution_bitcast_fusion = f32[32,2,16,16,128]{4,2,3,1,0:T(8,128)S(1)} fusion(f32[32,2,4,16,128]{4,3,2,1,0:T(8,128)S(1)} %convolution_bitcast_fusion.1, f32[32,16]{0,1:T(8,128)S(1)} %copy-done.5, s32[]{:T(128)S(6)} %select_n.6), kind=kOutput, calls=%fused_computation.5 | convolution fusion | flops 100663296 | bytes 10487812 | tf_op jit(solution)/shard_map/ipaso,ar->iprso/dot_general | solution.py:24
  21.4 8.3 %copy.73 = f32[32,2,16,16,128]{4,0,3,2,1:T(8,128)} copy(f32[32,2,16,16,128]{4,2,3,1,0:T(8,128)S(1)} %convolution_bitcast_fusion) | data formatting | bytes 16777216 | tf_op jit(solution)/shard_map/ipaso,ar->iprso/transpose | solution.py:24
  29.7 0.0 all-reduce.6.cloned.1.call-update
  29.7 0.0 all-reduce.4.cloned.1.call-start
  29.7 0.6 copy-done.7
  30.3 0.6 dynamic-slice
  31.5 105.1 %all-reduce.6.cloned.1.call-done = f32[32,2,16,16,128]{4,0,3,2,1:T(8,128)} async-done(((f32[32,2,16,16,128]{4,0,3,2,1:T(8,128)}), f32[32,2,16,16,128]{4,0,3,2,1:T(8,128)}) %all-reduce.6.cloned.1.call-update) | async-done | bytes 8388624
  136.6 9.3 %fusion.15 = f32[2,16,2,128,128]{4,3,2,1,0:T(8,128)} fusion(f32[32,2,16,16,128]{4,0,3,2,1:T(8,128)} %all-reduce.6.cloned.1.call-done, u32[]{:T(128)S(6)} %multiply.3, f32[32,128]{1,0:T(8,128)S(1)} %copy-done.4), kind=kOutput, calls=%fused_computation.14 | convolution fusion | flops 402653184 | bytes 5259268 | tf_op jit(solution)/shard_map/ik,iprso->kprso/dot_general | solution.py:26
  145.9 5.5 %copy.74 = f32[2,16,2,128,128]{3,1,2,0,4:T(8,128)} copy(f32[2,16,2,128,128]{4,3,2,1,0:T(8,128)} %fusion.15) | data formatting | bytes 8388608 | tf_op jit(solution)/shard_map/ik,iprso->kprso/dot_general | solution.py:26
  151.4 0.0 all-reduce.4.cloned.1.call-update
  151.4 0.0 all-gather.3.cloned.1.call-start
  151.5 103.7 %all-reduce.4.cloned.1.call-done = f32[128,2,16,2,128]{4,2,3,1,0:T(8,128)} async-done(((f32[128,2,16,2,128]{4,2,3,1,0:T(8,128)}), f32[128,2,16,2,128]{4,2,3,1,0:T(8,128)}) %all-reduce.4.cloned.1.call-update) | async-done | bytes 4194320 | tf_op jit(solution)/shard_map/psum | solution.py:26
  255.1 1.8 add_divide_fusion
  257.0 0.0 all-gather.3.cloned.1.call-update
  257.0 0.3 all-gather.5.cloned.1.call-start
  257.3 52.0 %all-gather.3.cloned.1.call-done = f32[128,2,16,2,128]{4,2,3,1,0:T(8,128)} async-done(((f32[8,2,16,2,128]{4,2,3,1,0:T(8,128)}), f32[128,2,16,2,128]{4,2,3,1,0:T(8,128)}) %all-gather.3.cloned.1.call-update) | async-done | bytes 4194320 | tf_op jit(solution)/shard_map/all_gather | solution.py:36
  309.3 6.8 %fusion.12 = f32[32,2,16,2,128]{4,0,3,2,1:T(8,128)S(1)} fusion(f32[128,2,16,2,128]{4,2,3,1,0:T(8,128)} %all-gather.3.cloned.1.call-done, f32[32,128]{1,0:T(8,128)S(1)} %copy-done.4), kind=kOutput, calls=%fused_computation.13 | convolution fusion | flops 402653184 | bytes 5259264 | tf_op jit(solution)/shard_map/ik,kprso->iprso/dot_general | solution.py:33
  316.1 1.6 copy.77
  317.7 0.0 all-gather.5.cloned.1.call-update
  317.7 0.8 copy.80
  318.6 0.8 copy.81
  319.4 48.3 %all-gather.5.cloned.1.call-done = f32[32,2,16,16,128]{4,2,1,0,3:T(8,128)} async-done(((f32[32,2,16,2,128]{4,2,1,0,3:T(8,128)}), f32[32,2,16,16,128]{4,2,1,0,3:T(8,128)}) %all-gather.5.cloned.1.call-update) | async-done | bytes 8388624 | tf_op jit(solution)/shard_map/all_gather | solution.py:39
  367.7 6.6 %fusion.9 = f32[32,2,4,16,128]{4,2,3,1,0:T(4,128)S(1)} fusion(f32[32,2,16,16,128]{4,2,1,0,3:T(8,128)} %all-gather.5.cloned.1.call-done, f32[32,16]{0,1:T(8,128)S(1)} %copy-done.5, s32[]{:T(128)S(6)} %select_n.6), kind=kOutput, calls=%fused_computation.11 | convolution fusion | flops 100663296 | bytes 10487812 | tf_op jit(solution)/shard_map/iprso,ar->ipaso/dot_general | solution.py:40
  374.3 0.0 copy-start.1
  374.3 3.7 fusion.5
  378.0 3.3 subtract_convert_fusion
  (11 shorter events, 0.0 us)
Async XLA Ops:
  7.2 0.8 copy-start
  7.2 129.5 %all-reduce.6.cloned.1.call-start = ((), (), s32[]{:S(2)}) async-start(), calls=%async_computation.3 | async-start | bytes 16777216
  8.0 3.4 copy-start.6
  11.5 2.3 copy-start.5
  29.6 0.7 copy-start.7
  29.6 107.0 %copy-start.4 = (f32[32,128]{1,0:T(8,128)S(1)}, f32[32,128]{1,0:T(8,128)}, u32[]{:S(2)}) copy-start(f32[32,128]{1,0:T(8,128)} %param.12) | copy-start | bytes 49156
  29.7 225.5 %all-reduce.4.cloned.1.call-start = ((), (), s32[]{:S(2)}) async-start(), calls=%async_computation | async-start | bytes 8388608 | tf_op jit(solution)/shard_map/psum | solution.py:26
  151.4 103.8 %copy-start.2 = (f32[8,2,16,2,128]{4,3,2,1,0:T(2,128)S(1)}, f32[8,2,16,2,128]{4,3,2,1,0:T(2,128)}, u32[]{:S(2)}) copy-start(f32[8,2,16,2,128]{4,3,2,1,0:T(2,128)} %param.10) | copy-start | bytes 786436
  151.4 103.8 %copy-start.3 = (f32[8,2,16,2,128]{4,3,2,1,0:T(2,128)S(1)}, f32[8,2,16,2,128]{4,3,2,1,0:T(2,128)}, u32[]{:S(2)}) copy-start(f32[8,2,16,2,128]{4,3,2,1,0:T(2,128)} %param.11) | copy-start | bytes 786436
  151.4 157.8 %all-gather.3.cloned.1.call-start = ((), (), s32[]{:S(2)}) async-start(), calls=%async_computation.1 | async-start | bytes 4456448 | tf_op jit(solution)/shard_map/all_gather | solution.py:36
  257.0 110.7 %all-gather.5.cloned.1.call-start = ((), (), s32[]{:S(2)}) async-start(), calls=%async_computation.2 | async-start | bytes 9437184 | tf_op jit(solution)/shard_map/all_gather | solution.py:39
  374.3 3.7 copy-start.1
Sparse Core Ops, SparseCore 0:
  29.8 106.7 all-reduce.5
  151.5 103.5 all-reduce.3
  257.9 51.3 all-gather.2
  317.8 49.8 all-gather.4
where the time goes:
time: 388 us
  waiting for transfers between devices  309 us (80%)
  matrix products  42.9 us (11%)
  local copies, waits for them, and re-layouts  19 us (5%)
  between operations  14.5 us (4%)
    unnamed x5, waiting for transfers between devices  105 us
    psum x1, waiting for transfers between devices, shards(): lax.psum(jnp.einsum('ik,iprso->kprso', u_in, mixed, precision=HIGH), 'chan')  104 us
    all_gather x1, waiting for transfers between devices, shards(): lax.all_gather(direction, 'chan', axis=0, tiled=True)  52 us
    all_gather x1, waiting for transfers between devices, shards(): full_ranks = lax.all_gather(spread, 'mode', axis=3, tiled=True)  48.3 us
    dot_general x1, matrix products, shards(): jnp.einsum('ik,iprso->kprso', u_in, mixed, precision=HIGH)  9.25 us
    transpose x1, local copies, waits for them, and re-layouts, shards(): jnp.einsum('ipaso,ar->iprso', narrowed, local_rows, precision=HIGH)  8.27 us
  transfers between devices with their start and end apart: 4, of which 4 were waited for; matrix products, arithmetic and copies ran while one was open for 1% of the time, Pallas kernels for 0%

commit v1 on v0

v1 whole, which is shorter than its diff:
```python
import jax
import jax.numpy as jnp
from jax import lax
from jax.experimental import pallas as pl
from jax.experimental.pallas import tpu as pltpu
from jax.sharding import PartitionSpec as P


STEP = 4
beta_one = 0.9
beta_two = 0.999
step_rate = 0.5

F32 = jnp.float32
BF16 = jnp.bfloat16
VMEM_LIMIT = 24 * 1024 * 1024
VMEM = pl.BlockSpec(memory_space=pltpu.VMEM)


def dot(a, b, dims=((1,), (0,))):
    return lax.dot_general(a, b, (dims, ((), ())), preferred_element_type=F32)


def split(x):
    hi = x.astype(BF16)
    return hi, (x - hi.astype(F32)).astype(BF16)


def dot3(a, b, dims=((1,), (0,))):
    return dot(a[0], b[0], dims) + (dot(a[0], b[1], dims) + dot(a[1], b[0], dims))


def swap_groups(tiles):
    lane = lax.broadcasted_iota(jnp.int32, tiles[0].shape, tiles[0].ndim - 1)
    axis = tiles[0].ndim - 1
    for bit in (1, 2, 4):
        upper = (lane & (16 * bit)) != 0
        out = list(tiles)
        for x in range(8):
            if x & bit:
                continue
            low, high = tiles[x], tiles[x + bit]
            out[x] = jnp.where(upper, pltpu.roll(high, 16 * bit, axis), low)
            out[x + bit] = jnp.where(upper, high, pltpu.roll(low, 128 - 16 * bit, axis))
        tiles = out
    return tiles


def one_hot(shape, row_of, col_of):
    rows = lax.broadcasted_iota(jnp.int32, shape, 0)
    cols = lax.broadcasted_iota(jnp.int32, shape, 1)
    return row_of(rows) == col_of(cols)


def spread_b(ub_t):
    rows = one_hot((128, 16), lambda r: r // 8, lambda c: c).astype(BF16)
    cols = one_hot((32, 256), lambda r: r, lambda c: c % 32).astype(BF16)
    same = one_hot((128, 256), lambda r: r % 8, lambda c: c // 32)
    return [
        jnp.where(same, dot(dot(rows, part).astype(BF16), cols), 0.0).astype(BF16)
        for part in split(ub_t)
    ]


def head_kernel(g_ref, uo_ref, ubt_ref, z_ref, kb_ref):
    @pl.when(pl.program_id(0) == 0)
    def _():
        hi, lo = spread_b(ubt_ref[...])
        kb_ref[0:128, :] = hi
        kb_ref[128:256, :] = lo

    kb = kb_ref[...]
    uo = uo_ref[...]
    for p in range(2):
        tiles = []
        for a in range(4):
            both = dot(kb, g_ref[:, p, a].reshape(256, 256))
            hi, lo = split(both[0:128] + both[128:256])
            nar = (dot(hi, uo) + dot(lo, uo)).reshape(8, 2, 8, 128)
            tiles += [nar[:, 0].reshape(64, 128), nar[:, 1].reshape(64, 128)]
        tiles = swap_groups(tiles)
        for j in range(8):
            z_ref[p * 8 + j] = tiles[j].reshape(8, 8, 128)


def head(gradient, u_out, ub_t):
    return pl.pallas_call(
        head_kernel,
        grid=(4,),
        in_specs=[
            pl.BlockSpec((8, 2, 4, 32, 256), lambda g: (g, 0, 0, 0, 0)),
            pl.BlockSpec((256, 128), lambda g: (0, 0)),
            pl.BlockSpec((16, 32), lambda g: (0, 0)),
        ],
        out_specs=pl.BlockSpec((16, 8, 8, 128), lambda g: (0, 0, g, 0)),
        out_shape=jax.ShapeDtypeStruct((16, 8, 32, 128), F32),
        scratch_shapes=[pltpu.VMEM((256, 256), BF16)],
        compiler_params=pltpu.CompilerParams(vmem_limit_bytes=54 * 1024 * 1024),
        name="head",
    )(gradient, u_out, ub_t)


def place(c, other):
    return (other // 4 + 4 - c // 4) % 4, (other % 4 + 4 - c % 4) % 4


def pack_kernel(fm_ref, sm_ref, ui_ref, o_ref):
    me = lax.axis_index("chan")
    for p in range(2):
        tiles = {}
        for which, ref in enumerate((fm_ref, sm_ref)):
            for q in range(4):
                tiles[which, q] = swap_groups([ref[:, p, q * 8 + x, :] for x in range(8)])
        for j in range(8):
            dz, dx = place(me, p * 8 + j)
            for which in range(2):
                for q in range(4):
                    at = which * 32 + q * 8
                    o_ref[dz, dx, at : at + 8, :] = tiles[which, q][j]
            o_ref[dz, dx, 64:96, :] = ui_ref[...]


def pack(fm, sm, u_in):
    return pl.pallas_call(
        pack_kernel,
        out_shape=jax.ShapeDtypeStruct((4, 4, 96, 128), F32),
        compiler_params=pltpu.CompilerParams(vmem_limit_bytes=VMEM_LIMIT),
        name="pack",
    )(fm, sm, u_in)


def exchange(blocks):
    rows = [blocks[0]]
    for d in range(1, 4):
        ring = [(c, (c // 4 + d) % 4 * 4 + c % 4) for c in range(16)]
        rows.append(lax.ppermute(blocks[d], "chan", ring))
    rows = jnp.stack(rows, axis=1)
    columns = [rows[0]]
    for d in range(1, 4):
        ring = [(c, c // 4 * 4 + (c % 4 + d) % 4) for c in range(16)]
        columns.append(lax.ppermute(rows[d], "chan", ring))
    return jnp.stack(columns)


def adam(core, fm, sm):
    new_first = beta_one * fm + (1.0 - beta_one) * core
    new_second = beta_two * sm + (1.0 - beta_two) * core * core
    return new_first, new_second


def prep_kernel(ua_ref, uat_ref, ka_ref, kat_ref):
    tall = one_hot((1024, 32), lambda r: r // 32, lambda c: c).astype(BF16)
    wide = one_hot((16, 512), lambda r: r, lambda c: c // 32).astype(BF16)
    same = one_hot((1024, 512), lambda r: r % 32, lambda c: c % 32)
    for n, part in enumerate(split(ua_ref[...])):
        ka_ref[n] = jnp.where(same, dot(dot(tall, part).astype(BF16), wide), 0.0).astype(BF16)
    tall = one_hot((512, 16), lambda r: r // 32, lambda c: c).astype(BF16)
    wide = one_hot((32, 1024), lambda r: r, lambda c: c // 32).astype(BF16)
    same = one_hot((512, 1024), lambda r: r % 32, lambda c: c % 32)
    for n, part in enumerate(split(uat_ref[...])):
        kat_ref[n] = jnp.where(same, dot(dot(tall, part).astype(BF16), wide), 0.0).astype(BF16)


def prep(u_a, u_at):
    return pl.pallas_call(
        prep_kernel,
        out_shape=(
            jax.ShapeDtypeStruct((2, 1024, 512), BF16),
            jax.ShapeDtypeStruct((2, 512, 1024), BF16),
        ),
        in_specs=[VMEM] * 2,
        out_specs=(VMEM, VMEM),
        compiler_params=pltpu.CompilerParams(vmem_limit_bytes=VMEM_LIMIT),
        name="prep",
    )(u_a, u_at)


def mid_kernel(x_ref, pk_ref, ka_ref, kat_ref, w_ref, core_ref):
    me = lax.axis_index("chan")

    def gathered(at, rows):
        parts = []
        for c in range(16):
            dz, dx = place(c, me)
            parts.append(pk_ref[dx, dz, at : at + rows, :])
        return jnp.concatenate(parts, axis=0)

    ui = gathered(64, 32)
    uit = split(ui.T)
    ui = split(ui)
    part = [dot3(uit, split(x_ref[:, m].reshape(512, 128))) for m in range(8)]
    part = split(jnp.concatenate(part, axis=1))
    core = dot3(part, (ka_ref[0], ka_ref[1]))
    dirs = []
    for q in range(4):
        mine = core[:, q * 128 : q * 128 + 128]
        for c in range(16):
            dz, dx = place(me, c)
            core_ref[dz, dx, q * 8 : q * 8 + 8, :] = mine[c * 8 : c * 8 + 8]
        new_first, new_second = adam(mine, gathered(q * 8, 8), gathered(32 + q * 8, 8))
        dirs.append(
            new_first / (1.0 - beta_one**STEP) / (jnp.sqrt(new_second / (1.0 - beta_two**STEP)) + 1e-08)
        )
    back = dot3(split(jnp.concatenate(dirs, axis=1)), (kat_ref[0], kat_ref[1]))
    for m in range(8):
        wide = dot3(ui, split(back[:, m * 128 : m * 128 + 128]))
        w_ref[:, m] = wide.reshape(16, 32, 128)


def mid(x, packed, ka, kat):
    return pl.pallas_call(
        mid_kernel,
        out_shape=(
            jax.ShapeDtypeStruct((16, 8, 32, 128), F32),
            jax.ShapeDtypeStruct((4, 4, 32, 128), F32),
        ),
        in_specs=[VMEM] * 4,
        out_specs=(VMEM, VMEM),
        compiler_params=pltpu.CompilerParams(vmem_limit_bytes=VMEM_LIMIT),
        name="mid",
    )(x, packed, ka, kat)


def moments_kernel(c_ref, fm_ref, sm_ref, nf_ref, ns_ref):
    me = lax.axis_index("chan")
    for p in range(2):
        at = [place(p * 8 + j, me) for j in range(8)]
        for q in range(4):
            tiles = swap_groups([c_ref[dx, dz, q * 8 : q * 8 + 8, :] for dz, dx in at])
            for x in range(8):
                s = q * 8 + x
                new_first, new_second = adam(tiles[x], fm_ref[:, p, s, :], sm_ref[:, p, s, :])
                nf_ref[:, p, s, :] = new_first
                ns_ref[:, p, s, :] = new_second


def moments(core, fm, sm):
    return pl.pallas_call(
        moments_kernel,
        out_shape=(jax.ShapeDtypeStruct(fm.shape, F32), jax.ShapeDtypeStruct(sm.shape, F32)),
        compiler_params=pltpu.CompilerParams(vmem_limit_bytes=VMEM_LIMIT),
        name="moments",
    )(core, fm, sm)


def tail_kernel(v_ref, w_ref, uo_ref, ubt_ref, o_ref, kb_ref):
    @pl.when(pl.program_id(0) == 0)
    def _():
        hi, lo = spread_b(ubt_ref[...])
        kb_ref[0] = hi.T
        kb_ref[1] = lo.T

    kb = (kb_ref[0], kb_ref[1])
    uo = uo_ref[...]
    rows = pl.ds(pl.program_id(0) * 8, 8)
    for p in range(2):
        tiles = swap_groups([v_ref[p * 8 + j, :, rows, :].reshape(64, 128) for j in range(8)])
        for a in range(4):
            wide = jnp.stack([t.reshape(8, 8, 128) for t in tiles[2 * a : 2 * a + 2]], axis=1)
            expanded = dot3(kb, split(wide.reshape(128, 128))).astype(BF16)
            update = dot(expanded, uo, ((1,), (1,))).reshape(8, 32, 256)
            o_ref[:, p, a] = (w_ref[:, p, a].astype(F32) - step_rate * update).astype(BF16)


def tail(v, weight, u_out, ub_t):
    return pl.pallas_call(
        tail_kernel,
        grid=(4,),
        in_specs=[
            VMEM,
            pl.BlockSpec((8, 2, 4, 32, 256), lambda g: (g, 0, 0, 0, 0)),
            pl.BlockSpec((256, 128), lambda g: (0, 0)),
            pl.BlockSpec((16, 32), lambda g: (0, 0)),
        ],
        out_specs=pl.BlockSpec((8, 2, 4, 32, 256), lambda g: (g, 0, 0, 0, 0)),
        out_shape=jax.ShapeDtypeStruct((32, 2, 4, 32, 256), BF16),
        scratch_shapes=[pltpu.VMEM((2, 256, 128), BF16)],
        compiler_params=pltpu.CompilerParams(vmem_limit_bytes=54 * 1024 * 1024),
        name="tail",
    )(v, weight, u_out, ub_t)


def shards(weight, gradient, first_moment, second_moment, u_in, u_out, u_modes_a, u_modes_b):
    both = ("chan", "mode")
    ub_t = u_modes_b.T
    fm = first_moment.reshape(8, 2, 32, 128)
    sm = second_moment.reshape(8, 2, 32, 128)
    sent = head(gradient, u_out, ub_t).reshape(128, 32, 128)
    got = lax.all_to_all(sent, both, 0, 0, tiled=True).reshape(16, 8, 32, 128)
    packed = exchange(pack(fm, sm, u_in))
    ka, kat = prep(u_modes_a, u_modes_a.T)
    wide, core = mid(got, packed, ka, kat)
    wide = lax.all_to_all(wide.reshape(128, 32, 128), both, 0, 0, tiled=True)
    core = exchange(core)
    new_first, new_second = moments(core, fm, sm)
    new_weight = tail(wide.reshape(16, 8, 32, 128), weight, u_out, ub_t)
    return new_weight, new_first.reshape(first_moment.shape), new_second.reshape(second_moment.shape)


def solution(mesh):
    in_specs = (
        P("chan", None, "mode", None, None),
        P("chan", None, "mode", None, None),
        P("chan", None, None, "mode", None),
        P("chan", None, None, "mode", None),
        P("chan", None),
        P(),
        P(),
        P(),
    )
    out_specs = (
        P("chan", None, "mode", None, None),
        P("chan", None, None, "mode", None),
        P("chan", None, None, "mode", None),
    )
    return jax.shard_map(shards, mesh=mesh, in_specs=in_specs, out_specs=out_specs, check_vma=False)
```

time: 388 us -> 139 us (0.36)
  waiting for transfers between devices: 309 us -> 65.6 us
  matrix products: 42.9 us -> 0 us
  starting transfers between devices: 0.38 us -> 32.1 us
  Pallas kernels: 0 us -> 28.4 us
  between operations: 14.5 us -> 0.81 us
  local copies, waits for them, and re-layouts: 19 us -> 10.2 us
    unnamed x5 -> x0, waiting for transfers between devices: 105 us -> none
    psum x1 -> x0, waiting for transfers between devices: 104 us -> none  [shards(): lax.psum(jnp.einsum('ik,iprso->kprso', u_in, mixed, precision=HIGH), 'chan')]
    all_gather x2 -> x0, waiting for transfers between devices: 100 us -> none  [the longest x1 52 us: shards(): lax.all_gather(direction, 'chan', axis=0, tiled=True)]
    ppermute x0 -> x12, waiting for transfers between devices: none -> 65.6 us  [the longest x6 54.1 us: exchange(): rows.append(lax.ppermute(blocks[d], 'chan', ring))]
    dot_general x8 -> x0, matrix products: 42.9 us -> none  [the longest x1 9.25 us: shards(): jnp.einsum('ik,iprso->kprso', u_in, mixed, precision=HIGH)]
    pallas_call x0 -> x6, Pallas kernels: none -> 28.4 us  [the longest x1 12.9 us: tail(): pl.pallas_call(tail_kernel, grid=(4,), in_specs=[VMEM, pl.BlockSpec((8, 2...]
    ppermute x0 -> x12, starting transfers between devices: none -> 16.3 us  [the longest x6 8.37 us: exchange(): rows.append(lax.ppermute(blocks[d], 'chan', ring))]
    all_to_all x0 -> x2, starting transfers between devices: none -> 15.8 us  [the longest x1 11.5 us: shards(): got = lax.all_to_all(sent, both, 0, 0, tiled=True).reshape(16, 8, 32, 128)]
  transfers between devices with their start and end apart: 4 -> 14, of which waited for: 4 -> 9; matrix products, arithmetic and copies ran while one was open for 1% -> 2% of each run, Pallas kernels for 0% -> 4%
where the time goes in v1:
time: 139 us
  waiting for transfers between devices  65.6 us (47%)
  starting transfers between devices  32.1 us (23%)
  Pallas kernels  28.4 us (20%)
  local copies, waits for them, and re-layouts  10.2 us (7%)
    ppermute x6, waiting for transfers between devices, exchange(): rows.append(lax.ppermute(blocks[d], 'chan', ring))  54.1 us
    pallas_call x1, Pallas kernels, tail(): pl.pallas_call(tail_kernel, grid=(4,), in_specs=[VMEM, pl.BlockSpec((8, 2...  12.9 us
    ppermute x6, waiting for transfers between devices, exchange(): columns.append(lax.ppermute(rows[d], 'chan', ring))  11.5 us
    all_to_all x1, starting transfers between devices, shards(): got = lax.all_to_all(sent, both, 0, 0, tiled=True).reshape(16, 8, 32, 128)  11.5 us
    unnamed x29, local copies, waits for them, and re-layouts  9.29 us
    ppermute x6, starting transfers between devices, exchange(): rows.append(lax.ppermute(blocks[d], 'chan', ring))  8.37 us
    ppermute x6, starting transfers between devices, exchange(): columns.append(lax.ppermute(rows[d], 'chan', ring))  7.91 us
    pallas_call x1, Pallas kernels, head(): pl.pallas_call(head_kernel, grid=(4,), in_specs=[pl.BlockSpec((8, 2, 4, 3...  7.45 us
  transfers between devices with their start and end apart: 14, of which 9 were waited for; matrix products, arithmetic and copies ran while one was open for 2% of the time, Pallas kernels for 4%

profile of v1, /device:TPU:1, one launch (start us, length us, event | category | flops | bytes accessed | tf_op | source)
XLA Modules:
  0.0 138.5 jit_solution(4633685222059827114)
XLA Ops:
  0.6 7.5 %head.1 = f32[16,8,32,128]{3,2,1,0:T(8,128)} custom-call(bf16[32,2,4,32,256]{4,3,2,1,0:T(8,128)(2,1)} %g_ref.1, bf16[256,128]{1,0:T(8,128)(2,1)} %uo_ref.3, f32[16,32]{1,0:T(8,128)} %bitcast.70), custom_call_target="tpu_custom_call" | custom-call | tf_op jit(solution)/shard_map/head/pallas_call | solution.py:87
  8.1 11.5 %all-to-all-start = ((f32[128,32,128]{2,1,0:T(8,128)}), f32[128,32,128]{2,1,0:T(8,128)S(1)}, u32[]{:S(2)}, u32[]{:S(2)}) async-start(f32[128,32,128]{2,1,0:T(8,128)} %bitcast.57), calls=%async_computation | async-start | bytes 4194304 | tf_op jit(solution)/shard_map/all_to_all | solution.py:289
  19.6 1.5 %pack.1 = f32[4,4,96,128]{3,2,1,0:T(8,128)S(1)} custom-call(f32[8,2,32,128]{3,2,1,0:T(8,128)S(1)} %bitcast.52, f32[8,2,32,128]{3,2,1,0:T(8,128)S(1)} %bitcast.54, f32[32,128]{1,0:T(8,128)S(1)} %copy-done.10), custom_call_target="tpu_custom_call" | custom-call | tf_op jit(solution)/shard_map/pack/pallas_call | solution.py:124
  21.2 3.3 %collective-permute-start.2 = (f32[4,96,128]{2,1,0:T(8,128)S(1)}, f32[4,96,128]{2,1,0:T(8,128)S(1)}, u32[]{:S(2)}, u32[]{:S(2)}) collective-permute-start(f32[4,96,128]{2,1,0:T(8,128)S(1)} %get-tuple-element.20), channel_id=1, source_target_pairs={{0,96},{8,104},{16,112},{24,120},{32,0},{40,8},{48,16},{56,24},{64... | collective-permute-start | bytes 589832 | tf_op jit(solution)/shard_map/ppermute | solution.py:136
  24.6 0.8 collective-permute-start
  25.3 23.0 %collective-permute-done.2 = f32[4,96,128]{2,1,0:T(8,128)S(1)} collective-permute-done((f32[4,96,128]{2,1,0:T(8,128)S(1)}, f32[4,96,128]{2,1,0:T(8,128)S(1)}, u32[]{:S(2)}, u32[]{:S(2)}) %collective-permute-start.2) | collective-permute-done | bytes 196640 | tf_op jit(solution)/shard_map/ppermute | solution.py:136
  48.3 1.6 %collective-permute-done.1 = f32[4,96,128]{2,1,0:T(8,128)S(1)} collective-permute-done((f32[4,96,128]{2,1,0:T(8,128)S(1)}, f32[4,96,128]{2,1,0:T(8,128)S(1)}, u32[]{:S(2)}, u32[]{:S(2)}) %collective-permute-start.1) | collective-permute-done | bytes 196640 | tf_op jit(solution)/shard_map/ppermute | solution.py:136
  49.9 5.0 %collective-permute-done = f32[4,96,128]{2,1,0:T(8,128)S(1)} collective-permute-done((f32[4,96,128]{2,1,0:T(8,128)S(1)}, f32[4,96,128]{2,1,0:T(8,128)S(1)}, u32[]{:S(2)}, u32[]{:S(2)}) %collective-permute-start) | collective-permute-done | bytes 196640 | tf_op jit(solution)/shard_map/ppermute | solution.py:136
  54.9 0.8 fusion
  55.7 2.5 %collective-permute-start.5 = (f32[4,96,128]{2,1,0:T(8,128)}, f32[4,96,128]{2,1,0:T(8,128)S(1)}, u32[]{:S(2)}, u32[]{:S(2)}) collective-permute-start(f32[4,96,128]{2,1,0:T(8,128)} %get-tuple-element.16), channel_id=1, source_target_pairs={{0,24},{8,0},{16,8},{24,16},{32,56},{40,32},{48,40},{56,48},{64,88... | collective-permute-start | bytes 589832 | tf_op jit(solution)/shard_map/ppermute | solution.py:141
  59.4 1.8 %prep.1 = (bf16[2,1024,512]{2,1,0:T(8,128)(2,1)S(1)}, bf16[2,512,1024]{2,1,0:T(8,128)(2,1)S(1)}) custom-call(f32[32,16]{1,0:T(8,128)S(1)} %copy.11.ua_ref, f32[16,32]{1,0:T(8,128)S(1)} %bitcast.56), custom_call_target="tpu_custom_call" | custom-call | tf_op jit(solution)/shard_map/prep/pallas_call | solution.py:165
  61.2 1.3 copy-done
  62.5 1.3 copy-done.2
  63.8 1.7 %collective-permute-done.4 = f32[4,96,128]{2,1,0:T(8,128)S(1)} collective-permute-done((f32[4,96,128]{2,1,0:T(8,128)S(1)}, f32[4,96,128]{2,1,0:T(8,128)S(1)}, u32[]{:S(2)}, u32[]{:S(2)}) %collective-permute-start.4) | collective-permute-done | bytes 196640 | tf_op jit(solution)/shard_map/ppermute | solution.py:141
  65.5 5.3 %collective-permute-done.3 = f32[4,96,128]{2,1,0:T(8,128)} collective-permute-done((f32[4,96,128]{2,1,0:T(8,128)S(1)}, f32[4,96,128]{2,1,0:T(8,128)}, u32[]{:S(2)}, u32[]{:S(2)}) %collective-permute-start.3) | collective-permute-done | bytes 196640 | tf_op jit(solution)/shard_map/ppermute | solution.py:141
  70.8 1.3 pad_maximum_fusion.1.pk_ref
  72.1 1.6 %copy-done.1 = bf16[2,1024,512]{2,1,0:T(8,128)(2,1)S(1)} copy-done((bf16[2,1024,512]{2,1,0:T(8,128)(2,1)S(1)}, bf16[2,1024,512]{2,1,0:T(8,128)(2,1)}, u32[]{:S(2)}) %copy-start.1) | copy-done | bytes 2097176
  73.7 1.6 %copy-done.3 = bf16[2,512,1024]{2,1,0:T(8,128)(2,1)S(1)} copy-done((bf16[2,512,1024]{2,1,0:T(8,128)(2,1)S(1)}, bf16[2,512,1024]{2,1,0:T(8,128)(2,1)}, u32[]{:S(2)}) %copy-start.3) | copy-done | bytes 2097176
  75.3 3.1 %mid.1 = (f32[16,8,32,128]{3,2,1,0:T(8,128)S(1)}, f32[4,4,32,128]{3,2,1,0:T(8,128)S(1)}) custom-call(f32[16,8,32,128]{3,2,1,0:T(8,128)S(1)} %bitcast.50, f32[4,4,96,128]{3,2,1,0:T(8,128)S(1)} %pad_maximum_fusion.1.pk_ref, bf16[2,1024,512]{2,1,0:T(8,128)(2,1)S(1)} %copy-done.1, bf16[2,512,1024]{2,1,0:T(8,128)(2,1)S(1)} %copy-done.3), custom_call_target="tpu_custom_call" | custom-call | tf_op jit(solution)/shard_map/mid/pallas_call | solution.py:211
  78.4 1.3 copy-done.4
  80.4 4.3 %all-to-all-start.1 = ((f32[128,32,128]{2,1,0:T(8,128)}), f32[128,32,128]{2,1,0:T(8,128)S(1)}, u32[]{:S(2)}, u32[]{:S(2)}) async-start(f32[128,32,128]{2,1,0:T(8,128)} %bitcast.51), calls=%async_computation.1 | async-start | bytes 4194304 | tf_op jit(solution)/shard_map/all_to_all | solution.py:293
  84.7 3.3 %collective-permute-start.8 = (f32[4,32,128]{2,1,0:T(8,128)S(1)}, f32[4,32,128]{2,1,0:T(8,128)S(1)}, u32[]{:S(2)}, u32[]{:S(2)}) collective-permute-start(f32[4,32,128]{2,1,0:T(8,128)S(1)} %get-tuple-element.28), channel_id=1, source_target_pairs={{0,96},{8,104},{16,112},{24,120},{32,0},{40,8},{48,16},{56,24},{64... | collective-permute-start | bytes 196616 | tf_op jit(solution)/shard_map/ppermute | solution.py:136
  88.2 0.8 collective-permute-start.6
  88.9 21.7 %collective-permute-done.8 = f32[4,32,128]{2,1,0:T(8,128)S(1)} collective-permute-done((f32[4,32,128]{2,1,0:T(8,128)S(1)}, f32[4,32,128]{2,1,0:T(8,128)S(1)}, u32[]{:S(2)}, u32[]{:S(2)}) %collective-permute-start.8) | collective-permute-done | bytes 65568 | tf_op jit(solution)/shard_map/ppermute | solution.py:136
  110.7 2.9 %collective-permute-done.6 = f32[4,32,128]{2,1,0:T(8,128)S(1)} collective-permute-done((f32[4,32,128]{2,1,0:T(8,128)S(1)}, f32[4,32,128]{2,1,0:T(8,128)S(1)}, u32[]{:S(2)}, u32[]{:S(2)}) %collective-permute-start.6) | collective-permute-done | bytes 65568 | tf_op jit(solution)/shard_map/ppermute | solution.py:136
  113.6 3.0 %collective-permute-start.11 = (f32[4,32,128]{2,1,0:T(8,128)S(1)}, f32[4,32,128]{2,1,0:T(8,128)S(1)}, u32[]{:S(2)}, u32[]{:S(2)}) collective-permute-start(f32[4,32,128]{2,1,0:T(8,128)S(1)} %get-tuple-element.24), channel_id=1, source_target_pairs={{0,24},{8,0},{16,8},{24,16},{32,56},{40,32},{48,40},{56,48},{64,88... | collective-permute-start | bytes 196616 | tf_op jit(solution)/shard_map/ppermute | solution.py:141
  117.1 0.8 collective-permute-start.9
  117.9 3.3 %collective-permute-done.10 = f32[4,32,128]{2,1,0:T(8,128)S(1)} collective-permute-done((f32[4,32,128]{2,1,0:T(8,128)S(1)}, f32[4,32,128]{2,1,0:T(8,128)S(1)}, u32[]{:S(2)}, u32[]{:S(2)}) %collective-permute-start.10) | collective-permute-done | bytes 65568 | tf_op jit(solution)/shard_map/ppermute | solution.py:141
  121.2 1.2 collective-permute-done.9
  122.4 1.8 %moments.1 = (f32[8,2,32,128]{3,2,1,0:T(8,128)}, f32[8,2,32,128]{3,2,1,0:T(8,128)}) custom-call(f32[4,4,32,128]{3,2,1,0:T(8,128)S(1)} %pad_maximum_fusion.3.c_ref, f32[8,2,32,128]{3,2,1,0:T(8,128)S(1)} %bitcast.53, f32[8,2,32,128]{3,2,1,0:T(8,128)S(1)} %bitcast.55), custom_call_target="tpu_custom_call" | custom-call | tf_op jit(solution)/shard_map/moments/pallas_call | solution.py:238
  124.3 1.3 copy-done.11
  125.6 12.9 %tail.1 = bf16[32,2,4,32,256]{4,3,2,1,0:T(8,128)(2,1)} custom-call(f32[16,8,32,128]{3,2,1,0:T(8,128)} %bitcast.58, bf16[32,2,4,32,256]{4,3,2,1,0:T(8,128)(2,1)} %w_ref.1, bf16[256,128]{1,0:T(8,128)(2,1)} %uo_ref.3, f32[16,32]{1,0:T(8,128)} %bitcast.71), custom_call_target="tpu_custom_call" | custom-call | tf_op jit(solution)/shard_map/tail/pallas_call | solution.py:266
  (39 shorter events, 3.0 us)
Async XLA Ops:
  8.1 11.5 %copy-start.5 = (f32[8,2,16,2,128]{4,3,2,1,0:T(2,128)S(1)}, f32[8,2,16,2,128]{4,3,2,1,0:T(2,128)}, u32[]{:S(2)}) copy-start(f32[8,2,16,2,128]{4,3,2,1,0:T(2,128)} %param.10) | copy-start | bytes 786436
  8.1 11.5 %copy-start.6 = (f32[8,2,16,2,128]{4,3,2,1,0:T(2,128)S(1)}, f32[8,2,16,2,128]{4,3,2,1,0:T(2,128)}, u32[]{:S(2)}) copy-start(f32[8,2,16,2,128]{4,3,2,1,0:T(2,128)} %param.11) | copy-start | bytes 786436
  8.1 11.5 %copy-start.10 = (f32[32,128]{1,0:T(8,128)S(1)}, f32[32,128]{1,0:T(8,128)}, u32[]{:S(2)}) copy-start(f32[32,128]{1,0:T(8,128)} %ui_ref.1) | copy-start | bytes 49156
  8.1 64.0 %all-to-all-start = ((f32[128,32,128]{2,1,0:T(8,128)}), f32[128,32,128]{2,1,0:T(8,128)S(1)}, u32[]{:S(2)}, u32[]{:S(2)}) async-start(f32[128,32,128]{2,1,0:T(8,128)} %bitcast.57), calls=%async_computation | async-start | bytes 4194304 | tf_op jit(solution)/shard_map/all_to_all | solution.py:289
  21.1 38.2 %copy-start.9 = (f32[32,16]{0,1:T(8,128)S(1)}, f32[32,16]{0,1:T(8,128)}, u32[]{:S(2)}) copy-start(f32[32,16]{0,1:T(8,128)} %param.14) | copy-start | bytes 6148
  21.2 27.2 %collective-permute-start.2 = (f32[4,96,128]{2,1,0:T(8,128)S(1)}, f32[4,96,128]{2,1,0:T(8,128)S(1)}, u32[]{:S(2)}, u32[]{:S(2)}) collective-permute-start(f32[4,96,128]{2,1,0:T(8,128)S(1)} %get-tuple-element.20), channel_id=1, source_target_pairs={{0,96},{8,104},{16,112},{24,120},{32,0},{40,8},{48,16},{56,24},{64... | collective-permute-start | bytes 589832 | tf_op jit(solution)/shard_map/ppermute | solution.py:136
  24.5 25.4 %collective-permute-start.1 = (f32[4,96,128]{2,1,0:T(8,128)S(1)}, f32[4,96,128]{2,1,0:T(8,128)S(1)}, u32[]{:S(2)}, u32[]{:S(2)}) collective-permute-start(f32[4,96,128]{2,1,0:T(8,128)S(1)} %get-tuple-element.21), channel_id=1, source_target_pairs={{0,64},{8,72},{16,80},{24,88},{32,96},{40,104},{48,112},{56,120},{... | collective-permute-start | bytes 589832 | tf_op jit(solution)/shard_map/ppermute | solution.py:136
  24.6 30.3 %collective-permute-start = (f32[4,96,128]{2,1,0:T(8,128)S(1)}, f32[4,96,128]{2,1,0:T(8,128)S(1)}, u32[]{:S(2)}, u32[]{:S(2)}) collective-permute-start(f32[4,96,128]{2,1,0:T(8,128)S(1)} %get-tuple-element.22), channel_id=1, source_target_pairs={{0,32},{8,40},{16,48},{24,56},{32,64},{40,72},{48,80},{56,88},{64,... | collective-permute-start | bytes 589832 | tf_op jit(solution)/shard_map/ppermute | solution.py:136
  55.7 8.1 %collective-permute-start.5 = (f32[4,96,128]{2,1,0:T(8,128)}, f32[4,96,128]{2,1,0:T(8,128)S(1)}, u32[]{:S(2)}, u32[]{:S(2)}) collective-permute-start(f32[4,96,128]{2,1,0:T(8,128)} %get-tuple-element.16), channel_id=1, source_target_pairs={{0,24},{8,0},{16,8},{24,16},{32,56},{40,32},{48,40},{56,48},{64,88... | collective-permute-start | bytes 589832 | tf_op jit(solution)/shard_map/ppermute | solution.py:141
  58.2 7.3 %collective-permute-start.4 = (f32[4,96,128]{2,1,0:T(8,128)S(1)}, f32[4,96,128]{2,1,0:T(8,128)S(1)}, u32[]{:S(2)}, u32[]{:S(2)}) collective-permute-start(f32[4,96,128]{2,1,0:T(8,128)S(1)} %get-tuple-element.17), channel_id=1, source_target_pairs={{0,16},{8,24},{16,0},{24,8},{32,48},{40,56},{48,32},{56,40},{64,80... | collective-permute-start | bytes 589832 | tf_op jit(solution)/shard_map/ppermute | solution.py:141
  58.7 12.2 %collective-permute-start.3 = (f32[4,96,128]{2,1,0:T(8,128)S(1)}, f32[4,96,128]{2,1,0:T(8,128)}, u32[]{:S(2)}, u32[]{:S(2)}) collective-permute-start(f32[4,96,128]{2,1,0:T(8,128)S(1)} %get-tuple-element.18), channel_id=1, source_target_pairs={{0,8},{8,16},{16,24},{24,0},{32,40},{40,48},{48,56},{56,32},{64,72... | collective-permute-start | bytes 589832 | tf_op jit(solution)/shard_map/ppermute | solution.py:141
  61.2 1.3 copy-start
  62.5 1.3 copy-start.2
  63.8 7.0 %copy-start.12 = (f32[4,96,128]{2,1,0:T(8,128)}, f32[4,96,128]{2,1,0:T(8,128)S(1)}, u32[]{:S(2)}) copy-start(f32[4,96,128]{2,1,0:T(8,128)S(1)} %collective-permute-done.5) | copy-start | bytes 589828
  65.5 5.3 %copy-start.13 = (f32[4,96,128]{2,1,0:T(8,128)}, f32[4,96,128]{2,1,0:T(8,128)S(1)}, u32[]{:S(2)}) copy-start(f32[4,96,128]{2,1,0:T(8,128)S(1)} %collective-permute-done.4) | copy-start | bytes 589828
  72.1 1.6 %copy-start.1 = (bf16[2,1024,512]{2,1,0:T(8,128)(2,1)S(1)}, bf16[2,1024,512]{2,1,0:T(8,128)(2,1)}, u32[]{:S(2)}) copy-start(bf16[2,1024,512]{2,1,0:T(8,128)(2,1)} %copy-done) | copy-start | bytes 6291460
  73.7 1.6 %copy-start.3 = (bf16[2,512,1024]{2,1,0:T(8,128)(2,1)S(1)}, bf16[2,512,1024]{2,1,0:T(8,128)(2,1)}, u32[]{:S(2)}) copy-start(bf16[2,512,1024]{2,1,0:T(8,128)(2,1)} %copy-done.2) | copy-start | bytes 6291460
  78.4 1.3 copy-start.4
  79.7 0.7 copy-start.7
  80.4 4.3 %copy-start.8 = (f32[4,4,32,128]{3,2,1,0:T(8,128)S(1)}, f32[4,4,32,128]{3,2,1,0:T(8,128)}, u32[]{:S(2)}) copy-start(f32[4,4,32,128]{3,2,1,0:T(8,128)} %copy-done.7) | copy-start | bytes 786436
  80.4 43.9 %all-to-all-start.1 = ((f32[128,32,128]{2,1,0:T(8,128)}), f32[128,32,128]{2,1,0:T(8,128)S(1)}, u32[]{:S(2)}, u32[]{:S(2)}) async-start(f32[128,32,128]{2,1,0:T(8,128)} %bitcast.51), calls=%async_computation.1 | async-start | bytes 4194304 | tf_op jit(solution)/shard_map/all_to_all | solution.py:293
  84.7 25.9 %collective-permute-start.8 = (f32[4,32,128]{2,1,0:T(8,128)S(1)}, f32[4,32,128]{2,1,0:T(8,128)S(1)}, u32[]{:S(2)}, u32[]{:S(2)}) collective-permute-start(f32[4,32,128]{2,1,0:T(8,128)S(1)} %get-tuple-element.28), channel_id=1, source_target_pairs={{0,96},{8,104},{16,112},{24,120},{32,0},{40,8},{48,16},{56,24},{64... | collective-permute-start | bytes 196616 | tf_op jit(solution)/shard_map/ppermute | solution.py:136
  88.0 22.6 %collective-permute-start.7 = (f32[4,32,128]{2,1,0:T(8,128)S(1)}, f32[4,32,128]{2,1,0:T(8,128)S(1)}, u32[]{:S(2)}, u32[]{:S(2)}) collective-permute-start(f32[4,32,128]{2,1,0:T(8,128)S(1)} %get-tuple-element.29), channel_id=1, source_target_pairs={{0,64},{8,72},{16,80},{24,88},{32,96},{40,104},{48,112},{56,120},{... | collective-permute-start | bytes 196616 | tf_op jit(solution)/shard_map/ppermute | solution.py:136
  88.2 25.4 %collective-permute-start.6 = (f32[4,32,128]{2,1,0:T(8,128)S(1)}, f32[4,32,128]{2,1,0:T(8,128)S(1)}, u32[]{:S(2)}, u32[]{:S(2)}) collective-permute-start(f32[4,32,128]{2,1,0:T(8,128)S(1)} %get-tuple-element.30), channel_id=1, source_target_pairs={{0,32},{8,40},{16,48},{24,56},{32,64},{40,72},{48,80},{56,88},{64,... | collective-permute-start | bytes 196616 | tf_op jit(solution)/shard_map/ppermute | solution.py:136
  113.6 4.3 %collective-permute-start.11 = (f32[4,32,128]{2,1,0:T(8,128)S(1)}, f32[4,32,128]{2,1,0:T(8,128)S(1)}, u32[]{:S(2)}, u32[]{:S(2)}) collective-permute-start(f32[4,32,128]{2,1,0:T(8,128)S(1)} %get-tuple-element.24), channel_id=1, source_target_pairs={{0,24},{8,0},{16,8},{24,16},{32,56},{40,32},{48,40},{56,48},{64,88... | collective-permute-start | bytes 196616 | tf_op jit(solution)/shard_map/ppermute | solution.py:141
  116.5 4.7 %collective-permute-start.10 = (f32[4,32,128]{2,1,0:T(8,128)S(1)}, f32[4,32,128]{2,1,0:T(8,128)S(1)}, u32[]{:S(2)}, u32[]{:S(2)}) collective-permute-start(f32[4,32,128]{2,1,0:T(8,128)S(1)} %get-tuple-element.25), channel_id=1, source_target_pairs={{0,16},{8,24},{16,0},{24,8},{32,48},{40,56},{48,32},{56,40},{64,80... | collective-permute-start | bytes 196616 | tf_op jit(solution)/shard_map/ppermute | solution.py:141
  117.1 5.3 %collective-permute-start.9 = (f32[4,32,128]{2,1,0:T(8,128)S(1)}, f32[4,32,128]{2,1,0:T(8,128)S(1)}, u32[]{:S(2)}, u32[]{:S(2)}) collective-permute-start(f32[4,32,128]{2,1,0:T(8,128)S(1)} %get-tuple-element.26), channel_id=1, source_target_pairs={{0,8},{8,16},{16,24},{24,0},{32,40},{40,48},{48,56},{56,32},{64,72... | collective-permute-start | bytes 196616 | tf_op jit(solution)/shard_map/ppermute | solution.py:141
  124.3 1.3 copy-start.11

commit v2 on v1

--- a/solution.py
+++ b/solution.py
@@ -15,6 +15,7 @@
 BF16 = jnp.bfloat16
 VMEM_LIMIT = 24 * 1024 * 1024
 VMEM = pl.BlockSpec(memory_space=pltpu.VMEM)
+HBM = pl.BlockSpec(memory_space=pltpu.HBM)
 
 
 def dot(a, b, dims=((1,), (0,))):
@@ -104,7 +105,7 @@
     return (other // 4 + 4 - c // 4) % 4, (other % 4 + 4 - c % 4) % 4
 
 
-def pack_kernel(fm_ref, sm_ref, ui_ref, o_ref):
+def pack_kernel(fm_ref, sm_ref, ui_ref, after_ref, o_ref):
     me = lax.axis_index("chan")
     for p in range(2):
         tiles = {}
@@ -120,13 +121,15 @@
             o_ref[dz, dx, 64:96, :] = ui_ref[...]
 
 
-def pack(fm, sm, u_in):
+def pack(fm, sm, u_in, after):
     return pl.pallas_call(
         pack_kernel,
+        in_specs=[VMEM, VMEM, VMEM, HBM],
+        out_specs=VMEM,
         out_shape=jax.ShapeDtypeStruct((4, 4, 96, 128), F32),
         compiler_params=pltpu.CompilerParams(vmem_limit_bytes=VMEM_LIMIT),
         name="pack",
-    )(fm, sm, u_in)
+    )(fm, sm, u_in, after)
 
 
 def exchange(blocks):
@@ -148,7 +151,7 @@
     return new_first, new_second
 
 
-def prep_kernel(ua_ref, uat_ref, ka_ref, kat_ref):
+def prep_kernel(ua_ref, uat_ref, ka_hbm, kat_hbm, ka_ref, kat_ref, sems):
     tall = one_hot((1024, 32), lambda r: r // 32, lambda c: c).astype(BF16)
     wide = one_hot((16, 512), lambda r: r, lambda c: c // 32).astype(BF16)
     same = one_hot((1024, 512), lambda r: r % 32, lambda c: c % 32)
@@ -159,6 +162,14 @@
     same = one_hot((512, 1024), lambda r: r % 32, lambda c: c % 32)
     for n, part in enumerate(split(uat_ref[...])):
         kat_ref[n] = jnp.where(same, dot(dot(tall, part).astype(BF16), wide), 0.0).astype(BF16)
+    copies = [
+        pltpu.make_async_copy(ka_ref, ka_hbm, sems.at[0]),
+        pltpu.make_async_copy(kat_ref, kat_hbm, sems.at[1]),
+    ]
+    for copy in copies:
+        copy.start()
+    for copy in copies:
+        copy.wait()
 
 
 def prep(u_a, u_at):
@@ -169,13 +180,22 @@
             jax.ShapeDtypeStruct((2, 512, 1024), BF16),
         ),
         in_specs=[VMEM] * 2,
-        out_specs=(VMEM, VMEM),
-        compiler_params=pltpu.CompilerParams(vmem_limit_bytes=VMEM_LIMIT),
+        out_specs=(HBM, HBM),
+        scratch_shapes=[
+            pltpu.VMEM((2, 1024, 512), BF16),
+            pltpu.VMEM((2, 512, 1024), BF16),
+            pltpu.SemaphoreType.DMA((2,)),
+        ],
+        compiler_params=pltpu.CompilerParams(vmem_limit_bytes=56 * 1024 * 1024),
         name="prep",
     )(u_a, u_at)
 
 
-def mid_kernel(x_ref, pk_ref, ka_ref, kat_ref, w_ref, core_ref):
+def mid_kernel(x_ref, pk_ref, ka_hbm, kat_hbm, old_hbm, w_hbm, core_ref, ka_ref, kat_ref, w_ref, sems):
+    ka_copy = pltpu.make_async_copy(ka_hbm, ka_ref, sems.at[8])
+    kat_copy = pltpu.make_async_copy(kat_hbm, kat_ref, sems.at[9])
+    ka_copy.start()
+    kat_copy.start()
     me = lax.axis_index("chan")
 
     def gathered(at, rows):
@@ -190,6 +210,7 @@
     ui = split(ui)
     part = [dot3(uit, split(x_ref[:, m].reshape(512, 128))) for m in range(8)]
     part = split(jnp.concatenate(part, axis=1))
+    ka_copy.wait()
     core = dot3(part, (ka_ref[0], ka_ref[1]))
     dirs = []
     for q in range(4):
@@ -201,24 +222,37 @@
         dirs.append(
             new_first / (1.0 - beta_one**STEP) / (jnp.sqrt(new_second / (1.0 - beta_two**STEP)) + 1e-08)
         )
+    kat_copy.wait()
     back = dot3(split(jnp.concatenate(dirs, axis=1)), (kat_ref[0], kat_ref[1]))
+    copies = []
     for m in range(8):
         wide = dot3(ui, split(back[:, m * 128 : m * 128 + 128]))
         w_ref[:, m] = wide.reshape(16, 32, 128)
-
-
-def mid(x, packed, ka, kat):
+        copies.append(pltpu.make_async_copy(w_ref.at[:, m], w_hbm.at[:, m], sems.at[m]))
+        copies[m].start()
+    for copy in copies:
+        copy.wait()
+
+
+def mid(x, packed, ka, kat, old):
     return pl.pallas_call(
         mid_kernel,
         out_shape=(
             jax.ShapeDtypeStruct((16, 8, 32, 128), F32),
             jax.ShapeDtypeStruct((4, 4, 32, 128), F32),
         ),
-        in_specs=[VMEM] * 4,
-        out_specs=(VMEM, VMEM),
-        compiler_params=pltpu.CompilerParams(vmem_limit_bytes=VMEM_LIMIT),
+        in_specs=[VMEM, VMEM, HBM, HBM, HBM],
+        out_specs=(HBM, VMEM),
+        scratch_shapes=[
+            pltpu.VMEM((2, 1024, 512), BF16),
+            pltpu.VMEM((2, 512, 1024), BF16),
+            pltpu.VMEM((16, 8, 32, 128), F32),
+            pltpu.SemaphoreType.DMA((10,)),
+        ],
+        compiler_params=pltpu.CompilerParams(vmem_limit_bytes=48 * 1024 * 1024),
+        input_output_aliases={4: 0},
         name="mid",
-    )(x, packed, ka, kat)
+    )(x, packed, ka, kat, old)
 
 
 def moments_kernel(c_ref, fm_ref, sm_ref, nf_ref, ns_ref):
@@ -247,19 +281,24 @@
     @pl.when(pl.program_id(0) == 0)
     def _():
         hi, lo = spread_b(ubt_ref[...])
-        kb_ref[0] = hi.T
-        kb_ref[1] = lo.T
-
-    kb = (kb_ref[0], kb_ref[1])
+        kb_ref[...] = jnp.concatenate([hi.T, hi.T, lo.T], axis=1)
+
+    kb = kb_ref[...]
     uo = uo_ref[...]
     rows = pl.ds(pl.program_id(0) * 8, 8)
     for p in range(2):
         tiles = swap_groups([v_ref[p * 8 + j, :, rows, :].reshape(64, 128) for j in range(8)])
-        for a in range(4):
-            wide = jnp.stack([t.reshape(8, 8, 128) for t in tiles[2 * a : 2 * a + 2]], axis=1)
-            expanded = dot3(kb, split(wide.reshape(128, 128))).astype(BF16)
-            update = dot(expanded, uo, ((1,), (1,))).reshape(8, 32, 256)
-            o_ref[:, p, a] = (w_ref[:, p, a].astype(F32) - step_rate * update).astype(BF16)
+        for pair in range(2):
+            wide = []
+            for a in (2 * pair, 2 * pair + 1):
+                both = [t.reshape(8, 8, 128) for t in tiles[2 * a : 2 * a + 2]]
+                wide.append(jnp.stack(both, axis=1).reshape(128, 128))
+            hi, lo = split(jnp.concatenate(wide, axis=1))
+            expanded = dot(kb, jnp.concatenate([hi, lo, hi], axis=0)).astype(BF16)
+            for n in range(2):
+                a = 2 * pair + n
+                update = dot(expanded[:, n * 128 : n * 128 + 128], uo, ((1,), (1,))).reshape(8, 32, 256)
+                o_ref[:, p, a] = (w_ref[:, p, a].astype(F32) - step_rate * update).astype(BF16)
 
 
 def tail(v, weight, u_out, ub_t):
@@ -274,8 +313,8 @@
         ],
         out_specs=pl.BlockSpec((8, 2, 4, 32, 256), lambda g: (g, 0, 0, 0, 0)),
         out_shape=jax.ShapeDtypeStruct((32, 2, 4, 32, 256), BF16),
-        scratch_shapes=[pltpu.VMEM((2, 256, 128), BF16)],
-        compiler_params=pltpu.CompilerParams(vmem_limit_bytes=54 * 1024 * 1024),
+        scratch_shapes=[pltpu.VMEM((256, 384), BF16)],
+        compiler_params=pltpu.CompilerParams(vmem_limit_bytes=48 * 1024 * 1024),
         name="tail",
     )(v, weight, u_out, ub_t)
 
@@ -287,9 +326,9 @@
     sm = second_moment.reshape(8, 2, 32, 128)
     sent = head(gradient, u_out, ub_t).reshape(128, 32, 128)
     got = lax.all_to_all(sent, both, 0, 0, tiled=True).reshape(16, 8, 32, 128)
-    packed = exchange(pack(fm, sm, u_in))
+    packed = exchange(pack(fm, sm, u_in, sent))
     ka, kat = prep(u_modes_a, u_modes_a.T)
-    wide, core = mid(got, packed, ka, kat)
+    wide, core = mid(got, packed, ka, kat, sent.reshape(got.shape))
     wide = lax.all_to_all(wide.reshape(128, 32, 128), both, 0, 0, tiled=True)
     core = exchange(core)
     new_first, new_second = moments(core, fm, sm)

time: 139 us -> 131 us (0.942)
  local copies, waits for them, and re-layouts: 10.2 us -> 2.3 us
    unnamed x29 -> x21, local copies, waits for them, and re-layouts: 9.29 us -> 1.41 us
    pallas_call x1, Pallas kernels: 12.9 us -> 7.64 us  [tail(): pl.pallas_call(tail_kernel, grid=(4,), in_specs=[VMEM, pl.BlockSpec((8, 2...]
    pallas_call x1, Pallas kernels: 3.05 us -> 5.56 us  [mid(): pl.pallas_call(mid_kernel, out_shape=(jax.ShapeDtypeStruct((16, 8, 32, 12...]
    pallas_call x1, Pallas kernels: 1.76 us -> 3.82 us  [prep(): pl.pallas_call(prep_kernel, out_shape=(jax.ShapeDtypeStruct((2, 1024, 512...]
  transfers between devices with their start and end apart: 14 -> 14, of which waited for: 9 -> 9; matrix products, arithmetic and copies ran while one was open for 2% -> 2% of each run, Pallas kernels for 4% -> 5%
where the time goes in v2:
time: 131 us; the launch traced here: 130 us
  waiting for transfers between devices  65.6 us (50%)
  starting transfers between devices  32 us (24%)
  Pallas kernels  27.8 us (21%)
  local copies, waits for them, and re-layouts  2.3 us (2%)
  other arithmetic  1.36 us (1%)
    ppermute x6, waiting for transfers between devices, exchange(): rows.append(lax.ppermute(blocks[d], 'chan', ring))  54.1 us
    ppermute x6, waiting for transfers between devices, exchange(): columns.append(lax.ppermute(rows[d], 'chan', ring))  11.5 us
    all_to_all x1, starting transfers between devices, shards(): got = lax.all_to_all(sent, both, 0, 0, tiled=True).reshape(16, 8, 32, 128)  11.5 us
    ppermute x6, starting transfers between devices, exchange(): rows.append(lax.ppermute(blocks[d], 'chan', ring))  8.37 us
    ppermute x6, starting transfers between devices, exchange(): columns.append(lax.ppermute(rows[d], 'chan', ring))  7.91 us
    pallas_call x1, Pallas kernels, tail(): pl.pallas_call(tail_kernel, grid=(4,), in_specs=[VMEM, pl.BlockSpec((8, 2...  7.64 us
    pallas_call x1, Pallas kernels, head(): pl.pallas_call(head_kernel, grid=(4,), in_specs=[pl.BlockSpec((8, 2, 4, 3...  7.46 us
    pallas_call x1, Pallas kernels, mid(): pl.pallas_call(mid_kernel, out_shape=(jax.ShapeDtypeStruct((16, 8, 32, 12...  5.56 us
  transfers between devices with their start and end apart: 14, of which 9 were waited for; matrix products, arithmetic and copies ran while one was open for 2% of the time, Pallas kernels for 5%

profile of v2, /device:TPU:1, one launch (start us, length us, event | category | flops | bytes accessed | tf_op | source)
XLA Modules:
  0.0 129.9 jit_solution(17558053582624057112)
XLA Ops:
  0.6 7.5 %head.1.old_hbm = f32[16,8,32,128]{3,2,1,0:T(8,128)} custom-call(bf16[32,2,4,32,256]{4,3,2,1,0:T(8,128)(2,1)} %g_ref.1, bf16[256,128]{1,0:T(8,128)(2,1)} %uo_ref.3, f32[16,32]{1,0:T(8,128)} %bitcast.56), custom_call_target="tpu_custom_call" | custom-call | tf_op jit(solution)/shard_map/head/pallas_call | solution.py:88
  8.1 11.5 %all-to-all-start = ((f32[128,32,128]{2,1,0:T(8,128)}), f32[128,32,128]{2,1,0:T(8,128)S(1)}, u32[]{:S(2)}, u32[]{:S(2)}) async-start(f32[128,32,128]{2,1,0:T(8,128)} %bitcast.1.after_ref), calls=%async_computation | async-start | bytes 4194304 | tf_op jit(solution)/shard_map/all_to_all | solution.py:328
  19.6 1.5 %pack.1 = f32[4,4,96,128]{3,2,1,0:T(8,128)S(1)} custom-call(f32[8,2,32,128]{3,2,1,0:T(8,128)S(1)} %bitcast.52, f32[8,2,32,128]{3,2,1,0:T(8,128)S(1)} %bitcast.54, f32[32,128]{1,0:T(8,128)S(1)} %copy-done.6, f32[128,32,128]{2,1,0:T(8,128)} %bitcast.1.after_ref), custom_call_target="tpu_custom_call" | custom-call | tf_op jit(solution)/shard_map/pack/pallas_call | solution.py:125
  21.2 3.3 %collective-permute-start.2 = (f32[4,96,128]{2,1,0:T(8,128)S(1)}, f32[4,96,128]{2,1,0:T(8,128)S(1)}, u32[]{:S(2)}, u32[]{:S(2)}) collective-permute-start(f32[4,96,128]{2,1,0:T(8,128)S(1)} %get-tuple-element.20), channel_id=1, source_target_pairs={{0,96},{8,104},{16,112},{24,120},{32,0},{40,8},{48,16},{56,24},{64... | collective-permute-start | bytes 589832 | tf_op jit(solution)/shard_map/ppermute | solution.py:139
  24.6 0.8 collective-permute-start
  25.3 23.0 %collective-permute-done.2 = f32[4,96,128]{2,1,0:T(8,128)S(1)} collective-permute-done((f32[4,96,128]{2,1,0:T(8,128)S(1)}, f32[4,96,128]{2,1,0:T(8,128)S(1)}, u32[]{:S(2)}, u32[]{:S(2)}) %collective-permute-start.2) | collective-permute-done | bytes 196640 | tf_op jit(solution)/shard_map/ppermute | solution.py:139
  48.3 1.6 %collective-permute-done.1 = f32[4,96,128]{2,1,0:T(8,128)S(1)} collective-permute-done((f32[4,96,128]{2,1,0:T(8,128)S(1)}, f32[4,96,128]{2,1,0:T(8,128)S(1)}, u32[]{:S(2)}, u32[]{:S(2)}) %collective-permute-start.1) | collective-permute-done | bytes 196640 | tf_op jit(solution)/shard_map/ppermute | solution.py:139
  49.9 5.0 %collective-permute-done = f32[4,96,128]{2,1,0:T(8,128)S(1)} collective-permute-done((f32[4,96,128]{2,1,0:T(8,128)S(1)}, f32[4,96,128]{2,1,0:T(8,128)S(1)}, u32[]{:S(2)}, u32[]{:S(2)}) %collective-permute-start) | collective-permute-done | bytes 196640 | tf_op jit(solution)/shard_map/ppermute | solution.py:139
  54.9 0.8 fusion
  55.7 2.5 %collective-permute-start.5 = (f32[4,96,128]{2,1,0:T(8,128)}, f32[4,96,128]{2,1,0:T(8,128)S(1)}, u32[]{:S(2)}, u32[]{:S(2)}) collective-permute-start(f32[4,96,128]{2,1,0:T(8,128)} %get-tuple-element.16), channel_id=1, source_target_pairs={{0,24},{8,0},{16,8},{24,16},{32,56},{40,32},{48,40},{56,48},{64,88... | collective-permute-start | bytes 589832 | tf_op jit(solution)/shard_map/ppermute | solution.py:144
  58.2 0.5 collective-permute-start.4
  58.7 0.7 collective-permute-start.3
  59.3 0.7 copy.12.ua_ref
  60.0 3.8 %prep.1 = (bf16[2,1024,512]{2,1,0:T(8,128)(2,1)}, bf16[2,512,1024]{2,1,0:T(8,128)(2,1)}) custom-call(f32[32,16]{1,0:T(8,128)} %copy.12.ua_ref, f32[16,32]{1,0:T(8,128)} %bitcast.69), custom_call_target="tpu_custom_call" | custom-call | tf_op jit(solution)/shard_map/prep/pallas_call | solution.py:176
  63.8 1.7 %collective-permute-done.4 = f32[4,96,128]{2,1,0:T(8,128)S(1)} collective-permute-done((f32[4,96,128]{2,1,0:T(8,128)S(1)}, f32[4,96,128]{2,1,0:T(8,128)S(1)}, u32[]{:S(2)}, u32[]{:S(2)}) %collective-permute-start.4) | collective-permute-done | bytes 196640 | tf_op jit(solution)/shard_map/ppermute | solution.py:144
  65.5 5.3 %collective-permute-done.3 = f32[4,96,128]{2,1,0:T(8,128)} collective-permute-done((f32[4,96,128]{2,1,0:T(8,128)S(1)}, f32[4,96,128]{2,1,0:T(8,128)}, u32[]{:S(2)}, u32[]{:S(2)}) %collective-permute-start.3) | collective-permute-done | bytes 196640 | tf_op jit(solution)/shard_map/ppermute | solution.py:144
  70.9 1.3 pad_maximum_fusion.1.pk_ref
  72.1 5.6 %mid.1 = (f32[16,8,32,128]{3,2,1,0:T(8,128)}, f32[4,4,32,128]{3,2,1,0:T(8,128)S(1)}) custom-call(f32[16,8,32,128]{3,2,1,0:T(8,128)S(1)} %bitcast.50, f32[4,4,96,128]{3,2,1,0:T(8,128)S(1)} %pad_maximum_fusion.1.pk_ref, bf16[2,1024,512]{2,1,0:T(8,128)(2,1)} %get-tuple-element.9.ka_hbm, ...), custom_call_target="tpu_custom_call", output_to_operand_aliasing={{0}: (4, {})} | custom-call | tf_op jit(solution)/shard_map/mid/pallas_call | solution.py:238
  77.7 0.7 copy-done.3
  78.4 4.3 %all-to-all-start.1 = ((f32[128,32,128]{2,1,0:T(8,128)}), f32[128,32,128]{2,1,0:T(8,128)S(1)}, u32[]{:S(2)}, u32[]{:S(2)}) async-start(f32[128,32,128]{2,1,0:T(8,128)} %bitcast.19), calls=%async_computation.1 | async-start | bytes 4194304 | tf_op jit(solution)/shard_map/all_to_all | solution.py:332
  82.8 3.3 %collective-permute-start.8 = (f32[4,32,128]{2,1,0:T(8,128)S(1)}, f32[4,32,128]{2,1,0:T(8,128)S(1)}, u32[]{:S(2)}, u32[]{:S(2)}) collective-permute-start(f32[4,32,128]{2,1,0:T(8,128)S(1)} %get-tuple-element.28), channel_id=1, source_target_pairs={{0,96},{8,104},{16,112},{24,120},{32,0},{40,8},{48,16},{56,24},{64... | collective-permute-start | bytes 196616 | tf_op jit(solution)/shard_map/ppermute | solution.py:139
  86.1 0.1 collective-permute-start.7
  86.2 0.8 collective-permute-start.6
  86.9 21.7 %collective-permute-done.8 = f32[4,32,128]{2,1,0:T(8,128)S(1)} collective-permute-done((f32[4,32,128]{2,1,0:T(8,128)S(1)}, f32[4,32,128]{2,1,0:T(8,128)S(1)}, u32[]{:S(2)}, u32[]{:S(2)}) %collective-permute-start.8) | collective-permute-done | bytes 65568 | tf_op jit(solution)/shard_map/ppermute | solution.py:139
  108.7 2.9 %collective-permute-done.6 = f32[4,32,128]{2,1,0:T(8,128)S(1)} collective-permute-done((f32[4,32,128]{2,1,0:T(8,128)S(1)}, f32[4,32,128]{2,1,0:T(8,128)S(1)}, u32[]{:S(2)}, u32[]{:S(2)}) %collective-permute-start.6) | collective-permute-done | bytes 65568 | tf_op jit(solution)/shard_map/ppermute | solution.py:139
  111.6 3.0 %collective-permute-start.11 = (f32[4,32,128]{2,1,0:T(8,128)S(1)}, f32[4,32,128]{2,1,0:T(8,128)S(1)}, u32[]{:S(2)}, u32[]{:S(2)}) collective-permute-start(f32[4,32,128]{2,1,0:T(8,128)S(1)} %get-tuple-element.24), channel_id=1, source_target_pairs={{0,24},{8,0},{16,8},{24,16},{32,56},{40,32},{48,40},{56,48},{64,88... | collective-permute-start | bytes 196616 | tf_op jit(solution)/shard_map/ppermute | solution.py:144
  114.5 0.6 collective-permute-start.10
  115.1 0.8 collective-permute-start.9
  115.9 3.3 %collective-permute-done.10 = f32[4,32,128]{2,1,0:T(8,128)S(1)} collective-permute-done((f32[4,32,128]{2,1,0:T(8,128)S(1)}, f32[4,32,128]{2,1,0:T(8,128)S(1)}, u32[]{:S(2)}, u32[]{:S(2)}) %collective-permute-start.10) | collective-permute-done | bytes 65568 | tf_op jit(solution)/shard_map/ppermute | solution.py:144
  119.2 1.2 collective-permute-done.9
  120.4 1.8 %moments.1 = (f32[8,2,32,128]{3,2,1,0:T(8,128)}, f32[8,2,32,128]{3,2,1,0:T(8,128)}) custom-call(f32[4,4,32,128]{3,2,1,0:T(8,128)S(1)} %pad_maximum_fusion.3.c_ref, f32[8,2,32,128]{3,2,1,0:T(8,128)S(1)} %bitcast.53, f32[8,2,32,128]{3,2,1,0:T(8,128)S(1)} %bitcast.55), custom_call_target="tpu_custom_call" | custom-call | tf_op jit(solution)/shard_map/moments/pallas_call | solution.py:272
  122.3 7.6 %tail.1 = bf16[32,2,4,32,256]{4,3,2,1,0:T(8,128)(2,1)} custom-call(f32[16,8,32,128]{3,2,1,0:T(8,128)S(1)} %bitcast.51, bf16[32,2,4,32,256]{4,3,2,1,0:T(8,128)(2,1)} %w_ref.1, bf16[256,128]{1,0:T(8,128)(2,1)S(1)} %copy-done.2, f32[16,32]{1,0:T(8,128)S(1)} %bitcast.57), custom_call_target="tpu_custom_call" | custom-call | tf_op jit(solution)/shard_map/tail/pallas_call | solution.py:305
  (31 shorter events, 0.4 us)
Async XLA Ops:
  8.1 11.5 %copy-start = (f32[8,2,16,2,128]{4,3,2,1,0:T(2,128)S(1)}, f32[8,2,16,2,128]{4,3,2,1,0:T(2,128)}, u32[]{:S(2)}) copy-start(f32[8,2,16,2,128]{4,3,2,1,0:T(2,128)} %param.10) | copy-start | bytes 786436
  8.1 11.5 %copy-start.1 = (f32[8,2,16,2,128]{4,3,2,1,0:T(2,128)S(1)}, f32[8,2,16,2,128]{4,3,2,1,0:T(2,128)}, u32[]{:S(2)}) copy-start(f32[8,2,16,2,128]{4,3,2,1,0:T(2,128)} %param.11) | copy-start | bytes 786436
  8.1 11.5 %copy-start.6 = (f32[32,128]{1,0:T(8,128)S(1)}, f32[32,128]{1,0:T(8,128)}, u32[]{:S(2)}) copy-start(f32[32,128]{1,0:T(8,128)} %ui_ref.1) | copy-start | bytes 49156
  8.1 64.0 %all-to-all-start = ((f32[128,32,128]{2,1,0:T(8,128)}), f32[128,32,128]{2,1,0:T(8,128)S(1)}, u32[]{:S(2)}, u32[]{:S(2)}) async-start(f32[128,32,128]{2,1,0:T(8,128)} %bitcast.1.after_ref), calls=%async_computation | async-start | bytes 4194304 | tf_op jit(solution)/shard_map/all_to_all | solution.py:328
  21.1 38.2 %copy-start.9 = (f32[32,16]{0,1:T(8,128)S(1)}, f32[32,16]{0,1:T(8,128)}, u32[]{:S(2)}) copy-start(f32[32,16]{0,1:T(8,128)} %param.14) | copy-start | bytes 6148
  21.2 27.2 %collective-permute-start.2 = (f32[4,96,128]{2,1,0:T(8,128)S(1)}, f32[4,96,128]{2,1,0:T(8,128)S(1)}, u32[]{:S(2)}, u32[]{:S(2)}) collective-permute-start(f32[4,96,128]{2,1,0:T(8,128)S(1)} %get-tuple-element.20), channel_id=1, source_target_pairs={{0,96},{8,104},{16,112},{24,120},{32,0},{40,8},{48,16},{56,24},{64... | collective-permute-start | bytes 589832 | tf_op jit(solution)/shard_map/ppermute | solution.py:139
  24.5 25.4 %collective-permute-start.1 = (f32[4,96,128]{2,1,0:T(8,128)S(1)}, f32[4,96,128]{2,1,0:T(8,128)S(1)}, u32[]{:S(2)}, u32[]{:S(2)}) collective-permute-start(f32[4,96,128]{2,1,0:T(8,128)S(1)} %get-tuple-element.21), channel_id=1, source_target_pairs={{0,64},{8,72},{16,80},{24,88},{32,96},{40,104},{48,112},{56,120},{... | collective-permute-start | bytes 589832 | tf_op jit(solution)/shard_map/ppermute | solution.py:139
  24.6 30.3 %collective-permute-start = (f32[4,96,128]{2,1,0:T(8,128)S(1)}, f32[4,96,128]{2,1,0:T(8,128)S(1)}, u32[]{:S(2)}, u32[]{:S(2)}) collective-permute-start(f32[4,96,128]{2,1,0:T(8,128)S(1)} %get-tuple-element.22), channel_id=1, source_target_pairs={{0,32},{8,40},{16,48},{24,56},{32,64},{40,72},{48,80},{56,88},{64,... | collective-permute-start | bytes 589832 | tf_op jit(solution)/shard_map/ppermute | solution.py:139
  55.7 8.1 %collective-permute-start.5 = (f32[4,96,128]{2,1,0:T(8,128)}, f32[4,96,128]{2,1,0:T(8,128)S(1)}, u32[]{:S(2)}, u32[]{:S(2)}) collective-permute-start(f32[4,96,128]{2,1,0:T(8,128)} %get-tuple-element.16), channel_id=1, source_target_pairs={{0,24},{8,0},{16,8},{24,16},{32,56},{40,32},{48,40},{56,48},{64,88... | collective-permute-start | bytes 589832 | tf_op jit(solution)/shard_map/ppermute | solution.py:144
  58.2 7.3 %collective-permute-start.4 = (f32[4,96,128]{2,1,0:T(8,128)S(1)}, f32[4,96,128]{2,1,0:T(8,128)S(1)}, u32[]{:S(2)}, u32[]{:S(2)}) collective-permute-start(f32[4,96,128]{2,1,0:T(8,128)S(1)} %get-tuple-element.17), channel_id=1, source_target_pairs={{0,16},{8,24},{16,0},{24,8},{32,48},{40,56},{48,32},{56,40},{64,80... | collective-permute-start | bytes 589832 | tf_op jit(solution)/shard_map/ppermute | solution.py:144
  58.7 12.2 %collective-permute-start.3 = (f32[4,96,128]{2,1,0:T(8,128)S(1)}, f32[4,96,128]{2,1,0:T(8,128)}, u32[]{:S(2)}, u32[]{:S(2)}) collective-permute-start(f32[4,96,128]{2,1,0:T(8,128)S(1)} %get-tuple-element.18), channel_id=1, source_target_pairs={{0,8},{8,16},{16,24},{24,0},{32,40},{40,48},{48,56},{56,32},{64,72... | collective-permute-start | bytes 589832 | tf_op jit(solution)/shard_map/ppermute | solution.py:144
  63.8 7.0 %copy-start.7 = (f32[4,96,128]{2,1,0:T(8,128)}, f32[4,96,128]{2,1,0:T(8,128)S(1)}, u32[]{:S(2)}) copy-start(f32[4,96,128]{2,1,0:T(8,128)S(1)} %collective-permute-done.5) | copy-start | bytes 589828
  65.5 5.3 %copy-start.8 = (f32[4,96,128]{2,1,0:T(8,128)}, f32[4,96,128]{2,1,0:T(8,128)S(1)}, u32[]{:S(2)}) copy-start(f32[4,96,128]{2,1,0:T(8,128)S(1)} %collective-permute-done.4) | copy-start | bytes 589828
  77.7 0.7 copy-start.3
  78.4 4.3 %copy-start.4 = (f32[4,4,32,128]{3,2,1,0:T(8,128)S(1)}, f32[4,4,32,128]{3,2,1,0:T(8,128)}, u32[]{:S(2)}) copy-start(f32[4,4,32,128]{3,2,1,0:T(8,128)} %copy-done.3) | copy-start | bytes 786436
  78.4 43.9 %all-to-all-start.1 = ((f32[128,32,128]{2,1,0:T(8,128)}), f32[128,32,128]{2,1,0:T(8,128)S(1)}, u32[]{:S(2)}, u32[]{:S(2)}) async-start(f32[128,32,128]{2,1,0:T(8,128)} %bitcast.19), calls=%async_computation.1 | async-start | bytes 4194304 | tf_op jit(solution)/shard_map/all_to_all | solution.py:332
  82.7 39.6 %copy-start.2 = (bf16[256,128]{1,0:T(8,128)(2,1)S(1)}, bf16[256,128]{1,0:T(8,128)(2,1)}, u32[]{:S(2)}) copy-start(bf16[256,128]{1,0:T(8,128)(2,1)} %uo_ref.3) | copy-start | bytes 196612
  82.7 39.6 %copy-start.5 = (f32[32,16]{0,1:T(8,128)S(1)}, f32[32,16]{0,1:T(8,128)}, u32[]{:S(2)}) copy-start(f32[32,16]{0,1:T(8,128)} %param.15) | copy-start | bytes 6148
  82.8 25.9 %collective-permute-start.8 = (f32[4,32,128]{2,1,0:T(8,128)S(1)}, f32[4,32,128]{2,1,0:T(8,128)S(1)}, u32[]{:S(2)}, u32[]{:S(2)}) collective-permute-start(f32[4,32,128]{2,1,0:T(8,128)S(1)} %get-tuple-element.28), channel_id=1, source_target_pairs={{0,96},{8,104},{16,112},{24,120},{32,0},{40,8},{48,16},{56,24},{64... | collective-permute-start | bytes 196616 | tf_op jit(solution)/shard_map/ppermute | solution.py:139
  86.1 22.6 %collective-permute-start.7 = (f32[4,32,128]{2,1,0:T(8,128)S(1)}, f32[4,32,128]{2,1,0:T(8,128)S(1)}, u32[]{:S(2)}, u32[]{:S(2)}) collective-permute-start(f32[4,32,128]{2,1,0:T(8,128)S(1)} %get-tuple-element.29), channel_id=1, source_target_pairs={{0,64},{8,72},{16,80},{24,88},{32,96},{40,104},{48,112},{56,120},{... | collective-permute-start | bytes 196616 | tf_op jit(solution)/shard_map/ppermute | solution.py:139
  86.2 25.4 %collective-permute-start.6 = (f32[4,32,128]{2,1,0:T(8,128)S(1)}, f32[4,32,128]{2,1,0:T(8,128)S(1)}, u32[]{:S(2)}, u32[]{:S(2)}) collective-permute-start(f32[4,32,128]{2,1,0:T(8,128)S(1)} %get-tuple-element.30), channel_id=1, source_target_pairs={{0,32},{8,40},{16,48},{24,56},{32,64},{40,72},{48,80},{56,88},{64,... | collective-permute-start | bytes 196616 | tf_op jit(solution)/shard_map/ppermute | solution.py:139
  111.6 4.3 %collective-permute-start.11 = (f32[4,32,128]{2,1,0:T(8,128)S(1)}, f32[4,32,128]{2,1,0:T(8,128)S(1)}, u32[]{:S(2)}, u32[]{:S(2)}) collective-permute-start(f32[4,32,128]{2,1,0:T(8,128)S(1)} %get-tuple-element.24), channel_id=1, source_target_pairs={{0,24},{8,0},{16,8},{24,16},{32,56},{40,32},{48,40},{56,48},{64,88... | collective-permute-start | bytes 196616 | tf_op jit(solution)/shard_map/ppermute | solution.py:144
  114.5 4.7 %collective-permute-start.10 = (f32[4,32,128]{2,1,0:T(8,128)S(1)}, f32[4,32,128]{2,1,0:T(8,128)S(1)}, u32[]{:S(2)}, u32[]{:S(2)}) collective-permute-start(f32[4,32,128]{2,1,0:T(8,128)S(1)} %get-tuple-element.25), channel_id=1, source_target_pairs={{0,16},{8,24},{16,0},{24,8},{32,48},{40,56},{48,32},{56,40},{64,80... | collective-permute-start | bytes 196616 | tf_op jit(solution)/shard_map/ppermute | solution.py:144
  115.1 5.3 %collective-permute-start.9 = (f32[4,32,128]{2,1,0:T(8,128)S(1)}, f32[4,32,128]{2,1,0:T(8,128)S(1)}, u32[]{:S(2)}, u32[]{:S(2)}) collective-permute-start(f32[4,32,128]{2,1,0:T(8,128)S(1)} %get-tuple-element.26), channel_id=1, source_target_pairs={{0,8},{8,16},{16,24},{24,0},{32,40},{40,48},{48,56},{56,32},{64,72... | collective-permute-start | bytes 196616 | tf_op jit(solution)/shard_map/ppermute | solution.py:144

commit v3 on v2

--- a/solution.py
+++ b/solution.py
@@ -101,10 +101,6 @@
     )(gradient, u_out, ub_t)
 
 
-def place(c, other):
-    return (other // 4 + 4 - c // 4) % 4, (other % 4 + 4 - c % 4) % 4
-
-
 def pack_kernel(fm_ref, sm_ref, ui_ref, after_ref, o_ref):
     me = lax.axis_index("chan")
     for p in range(2):
@@ -113,12 +109,12 @@
             for q in range(4):
                 tiles[which, q] = swap_groups([ref[:, p, q * 8 + x, :] for x in range(8)])
         for j in range(8):
-            dz, dx = place(me, p * 8 + j)
+            e, f = pair_steps(me, p * 8 + j)
             for which in range(2):
                 for q in range(4):
                     at = which * 32 + q * 8
-                    o_ref[dz, dx, at : at + 8, :] = tiles[which, q][j]
-            o_ref[dz, dx, 64:96, :] = ui_ref[...]
+                    o_ref[e, f, at : at + 8, :] = tiles[which, q][j]
+            o_ref[e, f, 64:96, :] = ui_ref[...]
 
 
 def pack(fm, sm, u_in, after):
@@ -126,23 +122,25 @@
         pack_kernel,
         in_specs=[VMEM, VMEM, VMEM, HBM],
         out_specs=VMEM,
-        out_shape=jax.ShapeDtypeStruct((4, 4, 96, 128), F32),
+        out_shape=jax.ShapeDtypeStruct((2, 8, 96, 128), F32),
         compiler_params=pltpu.CompilerParams(vmem_limit_bytes=VMEM_LIMIT),
         name="pack",
     )(fm, sm, u_in, after)
 
 
-def exchange(blocks):
-    rows = [blocks[0]]
-    for d in range(1, 4):
-        ring = [(c, (c // 4 + d) % 4 * 4 + c % 4) for c in range(16)]
-        rows.append(lax.ppermute(blocks[d], "chan", ring))
-    rows = jnp.stack(rows, axis=1)
-    columns = [rows[0]]
-    for d in range(1, 4):
-        ring = [(c, c // 4 * 4 + (c % 4 + d) % 4) for c in range(16)]
-        columns.append(lax.ppermute(rows[d], "chan", ring))
-    return jnp.stack(columns)
+def pair_steps(c, other):
+    shift = (other // 4 + 4 - c // 4) % 4 * 2 + (other // 2 + c // 2) % 2
+    return (other + c) % 2, shift
+
+
+def pair_exchange(blocks):
+    across = lax.ppermute(blocks[1], "chan", [(c, c ^ 1) for c in range(16)])
+    both = jnp.stack([blocks[0], across], axis=1)
+    got = [both[0]]
+    for f in range(1, 8):
+        ring = [(c, (c // 4 + f // 2) % 4 * 4 + (c % 4 + f % 2 * 2) % 4) for c in range(16)]
+        got.append(lax.ppermute(both[f], "chan", ring))
+    return got
 
 
 def adam(core, fm, sm):
@@ -151,17 +149,19 @@
     return new_first, new_second
 
 
-def prep_kernel(ua_ref, uat_ref, ka_hbm, kat_hbm, ka_ref, kat_ref, sems):
+def prep_kernel(uat_ref, ka_hbm, kat_hbm, ka_ref, kat_ref, sems):
     tall = one_hot((1024, 32), lambda r: r // 32, lambda c: c).astype(BF16)
     wide = one_hot((16, 512), lambda r: r, lambda c: c // 32).astype(BF16)
     same = one_hot((1024, 512), lambda r: r % 32, lambda c: c % 32)
-    for n, part in enumerate(split(ua_ref[...])):
-        ka_ref[n] = jnp.where(same, dot(dot(tall, part).astype(BF16), wide), 0.0).astype(BF16)
+    for n, part in enumerate(split(uat_ref[...])):
+        rows = dot(tall, part, ((1,), (1,))).astype(BF16)
+        ka_ref[n] = jnp.where(same, dot(rows, wide), 0.0).astype(BF16)
     tall = one_hot((512, 16), lambda r: r // 32, lambda c: c).astype(BF16)
     wide = one_hot((32, 1024), lambda r: r, lambda c: c // 32).astype(BF16)
     same = one_hot((512, 1024), lambda r: r % 32, lambda c: c % 32)
     for n, part in enumerate(split(uat_ref[...])):
-        kat_ref[n] = jnp.where(same, dot(dot(tall, part).astype(BF16), wide), 0.0).astype(BF16)
+        rows = dot(tall, part).astype(BF16)
+        kat_ref[n] = jnp.where(same, dot(rows, wide), 0.0).astype(BF16)
     copies = [
         pltpu.make_async_copy(ka_ref, ka_hbm, sems.at[0]),
         pltpu.make_async_copy(kat_ref, kat_hbm, sems.at[1]),
@@ -172,14 +172,14 @@
         copy.wait()
 
 
-def prep(u_a, u_at):
+def prep(u_at):
     return pl.pallas_call(
         prep_kernel,
         out_shape=(
             jax.ShapeDtypeStruct((2, 1024, 512), BF16),
             jax.ShapeDtypeStruct((2, 512, 1024), BF16),
         ),
-        in_specs=[VMEM] * 2,
+        in_specs=[VMEM],
         out_specs=(HBM, HBM),
         scratch_shapes=[
             pltpu.VMEM((2, 1024, 512), BF16),
@@ -188,10 +188,28 @@
         ],
         compiler_params=pltpu.CompilerParams(vmem_limit_bytes=56 * 1024 * 1024),
         name="prep",
-    )(u_a, u_at)
-
-
-def mid_kernel(x_ref, pk_ref, ka_hbm, kat_hbm, old_hbm, w_hbm, core_ref, ka_ref, kat_ref, w_ref, sems):
+    )(u_at)
+
+
+def collect_kernel(*refs):
+    for f in range(8):
+        refs[8][f] = refs[f][...]
+
+
+def collect(parts):
+    return pl.pallas_call(
+        collect_kernel,
+        out_shape=jax.ShapeDtypeStruct((8, 2, 96, 128), F32),
+        in_specs=[VMEM] * 8,
+        out_specs=VMEM,
+        compiler_params=pltpu.CompilerParams(vmem_limit_bytes=24 * 1024 * 1024),
+        name="collect",
+    )(*parts)
+
+
+def mid_kernel(
+    x_ref, ka_hbm, kat_hbm, old_hbm, pk_ref, w_hbm, core_ref, ka_ref, kat_ref, w_ref, sems
+):
     ka_copy = pltpu.make_async_copy(ka_hbm, ka_ref, sems.at[8])
     kat_copy = pltpu.make_async_copy(kat_hbm, kat_ref, sems.at[9])
     ka_copy.start()
@@ -201,23 +219,23 @@
     def gathered(at, rows):
         parts = []
         for c in range(16):
-            dz, dx = place(c, me)
-            parts.append(pk_ref[dx, dz, at : at + rows, :])
+            e, f = pair_steps(c, me)
+            parts.append(pk_ref[f, e, at : at + rows, :])
         return jnp.concatenate(parts, axis=0)
 
+    x = [split(x_ref[:, m].reshape(512, 128)) for m in range(8)]
     ui = gathered(64, 32)
     uit = split(ui.T)
     ui = split(ui)
-    part = [dot3(uit, split(x_ref[:, m].reshape(512, 128))) for m in range(8)]
-    part = split(jnp.concatenate(part, axis=1))
+    part = split(jnp.concatenate([dot3(uit, x[m]) for m in range(8)], axis=1))
     ka_copy.wait()
     core = dot3(part, (ka_ref[0], ka_ref[1]))
     dirs = []
     for q in range(4):
         mine = core[:, q * 128 : q * 128 + 128]
         for c in range(16):
-            dz, dx = place(me, c)
-            core_ref[dz, dx, q * 8 : q * 8 + 8, :] = mine[c * 8 : c * 8 + 8]
+            e, f = pair_steps(me, c)
+            core_ref[e, f, q * 8 : q * 8 + 8, :] = mine[c * 8 : c * 8 + 8]
         new_first, new_second = adam(mine, gathered(q * 8, 8), gathered(32 + q * 8, 8))
         dirs.append(
             new_first / (1.0 - beta_one**STEP) / (jnp.sqrt(new_second / (1.0 - beta_two**STEP)) + 1e-08)
@@ -239,9 +257,9 @@
         mid_kernel,
         out_shape=(
             jax.ShapeDtypeStruct((16, 8, 32, 128), F32),
-            jax.ShapeDtypeStruct((4, 4, 32, 128), F32),
+            jax.ShapeDtypeStruct((2, 8, 32, 128), F32),
         ),
-        in_specs=[VMEM, VMEM, HBM, HBM, HBM],
+        in_specs=[VMEM, HBM, HBM, HBM, VMEM],
         out_specs=(HBM, VMEM),
         scratch_shapes=[
             pltpu.VMEM((2, 1024, 512), BF16),
@@ -250,17 +268,20 @@
             pltpu.SemaphoreType.DMA((10,)),
         ],
         compiler_params=pltpu.CompilerParams(vmem_limit_bytes=48 * 1024 * 1024),
-        input_output_aliases={4: 0},
+        input_output_aliases={3: 0},
         name="mid",
-    )(x, packed, ka, kat, old)
-
-
-def moments_kernel(c_ref, fm_ref, sm_ref, nf_ref, ns_ref):
+    )(x, ka, kat, old, packed)
+
+
+def moments_kernel(fm_ref, sm_ref, *refs):
+    core, (nf_ref, ns_ref, c_ref) = refs[:8], refs[8:]
     me = lax.axis_index("chan")
+    for f in range(8):
+        c_ref[:, f] = core[f][...]
     for p in range(2):
-        at = [place(p * 8 + j, me) for j in range(8)]
+        at = [pair_steps(p * 8 + j, me) for j in range(8)]
         for q in range(4):
-            tiles = swap_groups([c_ref[dx, dz, q * 8 : q * 8 + 8, :] for dz, dx in at])
+            tiles = swap_groups([c_ref[e, f, q * 8 : q * 8 + 8, :] for e, f in at])
             for x in range(8):
                 s = q * 8 + x
                 new_first, new_second = adam(tiles[x], fm_ref[:, p, s, :], sm_ref[:, p, s, :])
@@ -272,9 +293,10 @@
     return pl.pallas_call(
         moments_kernel,
         out_shape=(jax.ShapeDtypeStruct(fm.shape, F32), jax.ShapeDtypeStruct(sm.shape, F32)),
+        scratch_shapes=[pltpu.VMEM((2, 8, 32, 128), F32)],
         compiler_params=pltpu.CompilerParams(vmem_limit_bytes=VMEM_LIMIT),
         name="moments",
-    )(core, fm, sm)
+    )(fm, sm, *core)
 
 
 def tail_kernel(v_ref, w_ref, uo_ref, ubt_ref, o_ref, kb_ref):
@@ -326,11 +348,11 @@
     sm = second_moment.reshape(8, 2, 32, 128)
     sent = head(gradient, u_out, ub_t).reshape(128, 32, 128)
     got = lax.all_to_all(sent, both, 0, 0, tiled=True).reshape(16, 8, 32, 128)
-    packed = exchange(pack(fm, sm, u_in, sent))
-    ka, kat = prep(u_modes_a, u_modes_a.T)
+    packed = collect(pair_exchange(pack(fm, sm, u_in, sent)))
+    ka, kat = prep(u_modes_a.T)
     wide, core = mid(got, packed, ka, kat, sent.reshape(got.shape))
     wide = lax.all_to_all(wide.reshape(128, 32, 128), both, 0, 0, tiled=True)
-    core = exchange(core)
+    core = pair_exchange(core)
     new_first, new_second = moments(core, fm, sm)
     new_weight = tail(wide.reshape(16, 8, 32, 128), weight, u_out, ub_t)
     return new_weight, new_first.reshape(first_moment.shape), new_second.reshape(second_moment.shape)

time: 131 us -> 144 us (1.099)
  starting transfers between devices: 32 us -> 51.8 us
  waiting for transfers between devices: 65.6 us -> 60.6 us
  local copies, waits for them, and re-layouts: 2.3 us -> 0.79 us
    ppermute x12 -> x16, starting transfers between devices: 16.3 us -> 30.6 us  [the longest x14 27.8 us: pair_exchange(): got.append(lax.ppermute(both[f], 'chan', ring))]
    all_to_all x1, starting transfers between devices: 4.27 us -> 9.68 us  [shards(): wide = lax.all_to_all(wide.reshape(128, 32, 128), both, 0, 0, tiled=True)]
    ppermute x12 -> x16, waiting for transfers between devices: 65.6 us -> 60.6 us  [the longest x2 54.4 us: pair_exchange(): across = lax.ppermute(blocks[1], 'chan', [(c, c ^ 1) for c in range(16)])]
  transfers between devices with their start and end apart: 14 -> 18, of which waited for: 9 -> 4; matrix products, arithmetic and copies ran while one was open for 2% -> 0% of each run, Pallas kernels for 5% -> 5%
where the time goes in v3:
time: 144 us; the launch traced here: 142 us
  waiting for transfers between devices  60.6 us (42%)
  starting transfers between devices  51.8 us (36%)
  Pallas kernels  27.8 us (19%)
    ppermute x2, waiting for transfers between devices, pair_exchange(): across = lax.ppermute(blocks[1], 'chan', [(c, c ^ 1) for c in range(16)])  54.4 us
    ppermute x14, starting transfers between devices, pair_exchange(): got.append(lax.ppermute(both[f], 'chan', ring))  27.8 us
    all_to_all x1, starting transfers between devices, shards(): got = lax.all_to_all(sent, both, 0, 0, tiled=True).reshape(16, 8, 32, 128)  11.5 us
    all_to_all x1, starting transfers between devices, shards(): wide = lax.all_to_all(wide.reshape(128, 32, 128), both, 0, 0, tiled=True)  9.68 us
    pallas_call x1, Pallas kernels, tail(): pl.pallas_call(tail_kernel, grid=(4,), in_specs=[VMEM, pl.BlockSpec((8, 2...  7.64 us
    pallas_call x1, Pallas kernels, head(): pl.pallas_call(head_kernel, grid=(4,), in_specs=[pl.BlockSpec((8, 2, 4, 3...  7.45 us
    ppermute x14, waiting for transfers between devices, pair_exchange(): got.append(lax.ppermute(both[f], 'chan', ring))  6.13 us
    pallas_call x1, Pallas kernels, mid(): pl.pallas_call(mid_kernel, out_shape=(jax.ShapeDtypeStruct((16, 8, 32, 12...  5.58 us
  transfers between devices with their start and end apart: 18, of which 4 were waited for; matrix products, arithmetic and copies ran while one was open for 0% of the time, Pallas kernels for 5%

profile of v3, /device:TPU:1, one launch (start us, length us, event | category | flops | bytes accessed | tf_op | source)
XLA Modules:
  0.0 141.9 jit_solution(14727822673079755074)
XLA Ops:
  0.6 7.5 %head.1.old_hbm = f32[16,8,32,128]{3,2,1,0:T(8,128)} custom-call(bf16[32,2,4,32,256]{4,3,2,1,0:T(8,128)(2,1)} %g_ref.1, bf16[256,128]{1,0:T(8,128)(2,1)} %uo_ref.3, f32[16,32]{1,0:T(8,128)} %bitcast.58), custom_call_target="tpu_custom_call" | custom-call | tf_op jit(solution)/shard_map/head/pallas_call | solution.py:88
  8.1 11.5 %all-to-all-start = ((f32[128,32,128]{2,1,0:T(8,128)}), f32[128,32,128]{2,1,0:T(8,128)S(1)}, u32[]{:S(2)}, u32[]{:S(2)}) async-start(f32[128,32,128]{2,1,0:T(8,128)} %bitcast.1.after_ref), calls=%async_computation | async-start | bytes 4194304 | tf_op jit(solution)/shard_map/all_to_all | solution.py:350
  19.6 1.5 %pack.1 = f32[2,8,96,128]{3,2,1,0:T(8,128)S(1)} custom-call(f32[8,2,32,128]{3,2,1,0:T(8,128)S(1)} %bitcast.54, f32[8,2,32,128]{3,2,1,0:T(8,128)S(1)} %bitcast.56, f32[32,128]{1,0:T(8,128)S(1)} %copy-done.6, f32[128,32,128]{2,1,0:T(8,128)} %bitcast.1.after_ref), custom_call_target="tpu_custom_call" | custom-call | tf_op jit(solution)/shard_map/pack/pallas_call | solution.py:121
  21.1 0.1 slice_bitcast_fusion
  21.1 1.4 %collective-permute-start = (f32[8,96,128]{2,1,0:T(8,128)S(1)}, f32[8,96,128]{2,1,0:T(8,128)S(1)}, u32[]{:S(2)}, u32[]{:S(2)}) collective-permute-start(f32[8,96,128]{2,1,0:T(8,128)S(1)} %get-tuple-element.23), channel_id=1, source_target_pairs={{0,8},{8,0},{16,24},{24,16},{32,40},{40,32},{48,56},{56,48},{64,72... | collective-permute-start | bytes 1179656 | tf_op jit(solution)/shard_map/ppermute | solution.py:137
  22.6 29.3 %collective-permute-done = f32[8,96,128]{2,1,0:T(8,128)S(1)} collective-permute-done((f32[8,96,128]{2,1,0:T(8,128)S(1)}, f32[8,96,128]{2,1,0:T(8,128)S(1)}, u32[]{:S(2)}, u32[]{:S(2)}) %collective-permute-start) | collective-permute-done | bytes 393248 | tf_op jit(solution)/shard_map/ppermute | solution.py:137
  51.8 0.1 fusion.14
  51.9 5.3 %collective-permute-start.7 = (f32[2,96,128]{2,1,0:T(8,128)S(1)}, f32[2,96,128]{2,1,0:T(8,128)S(1)}, u32[]{:S(2)}, u32[]{:S(2)}) collective-permute-start(f32[2,96,128]{2,1,0:T(8,128)S(1)} %get-tuple-element.15), channel_id=1, source_target_pairs={{0,112},{8,120},{16,96},{24,104},{32,16},{40,24},{48,0},{56,8},{64... | collective-permute-start | bytes 294920 | tf_op jit(solution)/shard_map/ppermute | solution.py:142
  57.2 0.5 collective-permute-start.1
  57.7 1.9 %collective-permute-start.3 = (f32[2,96,128]{2,1,0:T(8,128)S(1)}, f32[2,96,128]{2,1,0:T(8,128)S(1)}, u32[]{:S(2)}, u32[]{:S(2)}) collective-permute-start(f32[2,96,128]{2,1,0:T(8,128)S(1)} %get-tuple-element.19), channel_id=1, source_target_pairs={{0,48},{8,56},{16,32},{24,40},{32,80},{40,88},{48,64},{56,72},{64,... | collective-permute-start | bytes 294920 | tf_op jit(solution)/shard_map/ppermute | solution.py:142
  59.6 4.1 %collective-permute-start.4 = (f32[2,96,128]{2,1,0:T(8,128)S(1)}, f32[2,96,128]{2,1,0:T(8,128)S(1)}, u32[]{:S(2)}, u32[]{:S(2)}) collective-permute-start(f32[2,96,128]{2,1,0:T(8,128)S(1)} %get-tuple-element.20), channel_id=1, source_target_pairs={{0,64},{8,72},{16,80},{24,88},{32,96},{40,104},{48,112},{56,120},{... | collective-permute-start | bytes 294920 | tf_op jit(solution)/shard_map/ppermute | solution.py:142
  63.8 0.3 collective-permute-start.5
  64.0 0.0 collective-permute-done.1.refs_1_
  64.0 1.8 %collective-permute-start.6 = (f32[2,96,128]{2,1,0:T(8,128)S(1)}, f32[2,96,128]{2,1,0:T(8,128)S(1)}, u32[]{:S(2)}, u32[]{:S(2)}) collective-permute-start(f32[2,96,128]{2,1,0:T(8,128)S(1)} %get-tuple-element.22), channel_id=1, source_target_pairs={{0,96},{8,104},{16,112},{24,120},{32,0},{40,8},{48,16},{56,24},{64... | collective-permute-start | bytes 294920 | tf_op jit(solution)/shard_map/ppermute | solution.py:142
  65.8 3.8 %prep.1 = (bf16[2,1024,512]{2,1,0:T(8,128)(2,1)}, bf16[2,512,1024]{2,1,0:T(8,128)(2,1)}) custom-call(f32[16,32]{1,0:T(8,128)} %bitcast.62), custom_call_target="tpu_custom_call" | custom-call | tf_op jit(solution)/shard_map/prep/pallas_call | solution.py:176
  69.6 1.5 %collective-permute-done.5.refs_5_ = f32[2,96,128]{2,1,0:T(8,128)S(1)} collective-permute-done((f32[2,96,128]{2,1,0:T(8,128)S(1)}, f32[2,96,128]{2,1,0:T(8,128)S(1)}, u32[]{:S(2)}, u32[]{:S(2)}) %collective-permute-start.5) | collective-permute-done | bytes 98336 | tf_op jit(solution)/shard_map/ppermute | solution.py:142
  71.1 0.1 collect.1.pk_ref
  71.2 5.6 %mid.1 = (f32[16,8,32,128]{3,2,1,0:T(8,128)}, f32[2,8,32,128]{3,2,1,0:T(8,128)S(1)}) custom-call(f32[16,8,32,128]{3,2,1,0:T(8,128)S(1)} %bitcast.52, bf16[2,1024,512]{2,1,0:T(8,128)(2,1)} %get-tuple-element.9.ka_hbm, bf16[2,512,1024]{2,1,0:T(8,128)(2,1)} %get-tuple-element.10.kat_hbm, ...), custom_call_target="tpu_custom_call", output_to_operand_aliasing={{0}: (3, {})} | custom-call | tf_op jit(solution)/shard_map/mid/pallas_call | solution.py:256
  76.8 0.0 copy-start.3
  76.8 0.7 copy-done.3
  77.5 9.7 %all-to-all-start.1 = ((f32[128,32,128]{2,1,0:T(8,128)}), f32[128,32,128]{2,1,0:T(8,128)S(1)}, u32[]{:S(2)}, u32[]{:S(2)}) async-start(f32[128,32,128]{2,1,0:T(8,128)} %bitcast.17), calls=%async_computation.1 | async-start | bytes 4194304 | tf_op jit(solution)/shard_map/all_to_all | solution.py:354
  87.2 1.4 %collective-permute-start.8 = (f32[8,32,128]{2,1,0:T(8,128)S(1)}, f32[8,32,128]{2,1,0:T(8,128)S(1)}, u32[]{:S(2)}, u32[]{:S(2)}) collective-permute-start(f32[8,32,128]{2,1,0:T(8,128)S(1)} %get-tuple-element.33), channel_id=1, source_target_pairs={{0,8},{8,0},{16,24},{24,16},{32,40},{40,32},{48,56},{56,48},{64,72... | collective-permute-start | bytes 393224 | tf_op jit(solution)/shard_map/ppermute | solution.py:137
  88.7 25.2 %collective-permute-done.8 = f32[8,32,128]{2,1,0:T(8,128)S(1)} collective-permute-done((f32[8,32,128]{2,1,0:T(8,128)S(1)}, f32[8,32,128]{2,1,0:T(8,128)S(1)}, u32[]{:S(2)}, u32[]{:S(2)}) %collective-permute-start.8) | collective-permute-done | bytes 131104 | tf_op jit(solution)/shard_map/ppermute | solution.py:137
  113.8 5.3 %collective-permute-start.15 = (f32[2,32,128]{2,1,0:T(8,128)S(1)}, f32[2,32,128]{2,1,0:T(8,128)S(1)}, u32[]{:S(2)}, u32[]{:S(2)}) collective-permute-start(f32[2,32,128]{2,1,0:T(8,128)S(1)} %get-tuple-element.25), channel_id=1, source_target_pairs={{0,112},{8,120},{16,96},{24,104},{32,16},{40,24},{48,0},{56,8},{64... | collective-permute-start | bytes 98312 | tf_op jit(solution)/shard_map/ppermute | solution.py:142
  119.1 0.5 collective-permute-start.9
  119.7 1.9 %collective-permute-start.11 = (f32[2,32,128]{2,1,0:T(8,128)S(1)}, f32[2,32,128]{2,1,0:T(8,128)S(1)}, u32[]{:S(2)}, u32[]{:S(2)}) collective-permute-start(f32[2,32,128]{2,1,0:T(8,128)S(1)} %get-tuple-element.29), channel_id=1, source_target_pairs={{0,48},{8,56},{16,32},{24,40},{32,80},{40,88},{48,64},{56,72},{64,... | collective-permute-start | bytes 98312 | tf_op jit(solution)/shard_map/ppermute | solution.py:142
  121.5 4.1 %collective-permute-start.12 = (f32[2,32,128]{2,1,0:T(8,128)S(1)}, f32[2,32,128]{2,1,0:T(8,128)S(1)}, u32[]{:S(2)}, u32[]{:S(2)}) collective-permute-start(f32[2,32,128]{2,1,0:T(8,128)S(1)} %get-tuple-element.30), channel_id=1, source_target_pairs={{0,64},{8,72},{16,80},{24,88},{32,96},{40,104},{48,112},{56,120},{... | collective-permute-start | bytes 98312 | tf_op jit(solution)/shard_map/ppermute | solution.py:142
  125.7 0.3 collective-permute-start.13
  126.0 1.8 %collective-permute-start.14 = (f32[2,32,128]{2,1,0:T(8,128)S(1)}, f32[2,32,128]{2,1,0:T(8,128)S(1)}, u32[]{:S(2)}, u32[]{:S(2)}) collective-permute-start(f32[2,32,128]{2,1,0:T(8,128)S(1)} %get-tuple-element.32), channel_id=1, source_target_pairs={{0,96},{8,104},{16,112},{24,120},{32,0},{40,8},{48,16},{56,24},{64... | collective-permute-start | bytes 98312 | tf_op jit(solution)/shard_map/ppermute | solution.py:142
  127.8 4.6 %collective-permute-done.13.refs_5_ = f32[2,32,128]{2,1,0:T(8,128)S(1)} collective-permute-done((f32[2,32,128]{2,1,0:T(8,128)S(1)}, f32[2,32,128]{2,1,0:T(8,128)S(1)}, u32[]{:S(2)}, u32[]{:S(2)}) %collective-permute-start.13) | collective-permute-done | bytes 32800 | tf_op jit(solution)/shard_map/ppermute | solution.py:142
  132.4 1.9 %moments.1 = (f32[8,2,32,128]{3,2,1,0:T(8,128)}, f32[8,2,32,128]{3,2,1,0:T(8,128)}) custom-call(f32[8,2,32,128]{3,2,1,0:T(8,128)S(1)} %bitcast.55, f32[8,2,32,128]{3,2,1,0:T(8,128)S(1)} %bitcast.57, f32[2,32,128]{2,1,0:T(8,128)S(1)} %get-tuple-element.26.refs_0_, f32[2,32,128]{2,1,0:T(8,128)S(1)} %collective-permute-done.9.refs_1_, ...), custom_call_target="tpu_custom_call" | custom-call | tf_op jit(solution)/shard_map/moments/pallas_call | solution.py:293
  134.2 7.6 %tail.1 = bf16[32,2,4,32,256]{4,3,2,1,0:T(8,128)(2,1)} custom-call(f32[16,8,32,128]{3,2,1,0:T(8,128)S(1)} %bitcast.53, bf16[32,2,4,32,256]{4,3,2,1,0:T(8,128)(2,1)} %w_ref.1, bf16[256,128]{1,0:T(8,128)(2,1)S(1)} %copy-done.2, f32[16,32]{1,0:T(8,128)S(1)} %bitcast.59), custom_call_target="tpu_custom_call" | custom-call | tf_op jit(solution)/shard_map/tail/pallas_call | solution.py:327
  (29 shorter events, 0.1 us)
Async XLA Ops:
  8.1 11.5 %copy-start = (f32[8,2,16,2,128]{4,3,2,1,0:T(2,128)S(1)}, f32[8,2,16,2,128]{4,3,2,1,0:T(2,128)}, u32[]{:S(2)}) copy-start(f32[8,2,16,2,128]{4,3,2,1,0:T(2,128)} %param.10) | copy-start | bytes 786436
  8.1 11.5 %copy-start.1 = (f32[8,2,16,2,128]{4,3,2,1,0:T(2,128)S(1)}, f32[8,2,16,2,128]{4,3,2,1,0:T(2,128)}, u32[]{:S(2)}) copy-start(f32[8,2,16,2,128]{4,3,2,1,0:T(2,128)} %param.11) | copy-start | bytes 786436
  8.1 11.5 %copy-start.6 = (f32[32,128]{1,0:T(8,128)S(1)}, f32[32,128]{1,0:T(8,128)}, u32[]{:S(2)}) copy-start(f32[32,128]{1,0:T(8,128)} %ui_ref.1) | copy-start | bytes 49156
  8.1 63.1 %all-to-all-start = ((f32[128,32,128]{2,1,0:T(8,128)}), f32[128,32,128]{2,1,0:T(8,128)S(1)}, u32[]{:S(2)}, u32[]{:S(2)}) async-start(f32[128,32,128]{2,1,0:T(8,128)} %bitcast.1.after_ref), calls=%async_computation | async-start | bytes 4194304 | tf_op jit(solution)/shard_map/all_to_all | solution.py:350
  21.1 30.7 %collective-permute-start = (f32[8,96,128]{2,1,0:T(8,128)S(1)}, f32[8,96,128]{2,1,0:T(8,128)S(1)}, u32[]{:S(2)}, u32[]{:S(2)}) collective-permute-start(f32[8,96,128]{2,1,0:T(8,128)S(1)} %get-tuple-element.23), channel_id=1, source_target_pairs={{0,8},{8,0},{16,24},{24,16},{32,40},{40,32},{48,56},{56,48},{64,72... | collective-permute-start | bytes 1179656 | tf_op jit(solution)/shard_map/ppermute | solution.py:137
  51.9 11.8 %collective-permute-start.7 = (f32[2,96,128]{2,1,0:T(8,128)S(1)}, f32[2,96,128]{2,1,0:T(8,128)S(1)}, u32[]{:S(2)}, u32[]{:S(2)}) collective-permute-start(f32[2,96,128]{2,1,0:T(8,128)S(1)} %get-tuple-element.15), channel_id=1, source_target_pairs={{0,112},{8,120},{16,96},{24,104},{32,16},{40,24},{48,0},{56,8},{64... | collective-permute-start | bytes 294920 | tf_op jit(solution)/shard_map/ppermute | solution.py:142
  57.2 6.8 %collective-permute-start.1 = (f32[2,96,128]{2,1,0:T(8,128)S(1)}, f32[2,96,128]{2,1,0:T(8,128)S(1)}, u32[]{:S(2)}, u32[]{:S(2)}) collective-permute-start(f32[2,96,128]{2,1,0:T(8,128)S(1)} %get-tuple-element.17), channel_id=1, source_target_pairs={{0,16},{8,24},{16,0},{24,8},{32,48},{40,56},{48,32},{56,40},{64,80... | collective-permute-start | bytes 294920 | tf_op jit(solution)/shard_map/ppermute | solution.py:142
  57.7 11.9 %collective-permute-start.2 = (f32[2,96,128]{2,1,0:T(8,128)S(1)}, f32[2,96,128]{2,1,0:T(8,128)S(1)}, u32[]{:S(2)}, u32[]{:S(2)}) collective-permute-start(f32[2,96,128]{2,1,0:T(8,128)S(1)} %get-tuple-element.18), channel_id=1, source_target_pairs={{0,32},{8,40},{16,48},{24,56},{32,64},{40,72},{48,80},{56,88},{64,... | collective-permute-start | bytes 294920 | tf_op jit(solution)/shard_map/ppermute | solution.py:142
  57.7 11.9 %collective-permute-start.3 = (f32[2,96,128]{2,1,0:T(8,128)S(1)}, f32[2,96,128]{2,1,0:T(8,128)S(1)}, u32[]{:S(2)}, u32[]{:S(2)}) collective-permute-start(f32[2,96,128]{2,1,0:T(8,128)S(1)} %get-tuple-element.19), channel_id=1, source_target_pairs={{0,48},{8,56},{16,32},{24,40},{32,80},{40,88},{48,64},{56,72},{64,... | collective-permute-start | bytes 294920 | tf_op jit(solution)/shard_map/ppermute | solution.py:142
  59.6 10.0 %collective-permute-start.4 = (f32[2,96,128]{2,1,0:T(8,128)S(1)}, f32[2,96,128]{2,1,0:T(8,128)S(1)}, u32[]{:S(2)}, u32[]{:S(2)}) collective-permute-start(f32[2,96,128]{2,1,0:T(8,128)S(1)} %get-tuple-element.20), channel_id=1, source_target_pairs={{0,64},{8,72},{16,80},{24,88},{32,96},{40,104},{48,112},{56,120},{... | collective-permute-start | bytes 294920 | tf_op jit(solution)/shard_map/ppermute | solution.py:142
  63.8 7.4 %collective-permute-start.5 = (f32[2,96,128]{2,1,0:T(8,128)S(1)}, f32[2,96,128]{2,1,0:T(8,128)S(1)}, u32[]{:S(2)}, u32[]{:S(2)}) collective-permute-start(f32[2,96,128]{2,1,0:T(8,128)S(1)} %get-tuple-element.21), channel_id=1, source_target_pairs={{0,80},{8,88},{16,64},{24,72},{32,112},{40,120},{48,96},{56,104},{... | collective-permute-start | bytes 294920 | tf_op jit(solution)/shard_map/ppermute | solution.py:142
  64.0 7.1 %collective-permute-start.6 = (f32[2,96,128]{2,1,0:T(8,128)S(1)}, f32[2,96,128]{2,1,0:T(8,128)S(1)}, u32[]{:S(2)}, u32[]{:S(2)}) collective-permute-start(f32[2,96,128]{2,1,0:T(8,128)S(1)} %get-tuple-element.22), channel_id=1, source_target_pairs={{0,96},{8,104},{16,112},{24,120},{32,0},{40,8},{48,16},{56,24},{64... | collective-permute-start | bytes 294920 | tf_op jit(solution)/shard_map/ppermute | solution.py:142
  76.8 0.7 copy-start.3
  77.5 9.7 %copy-start.4 = (f32[2,8,32,128]{3,2,1,0:T(8,128)S(1)}, f32[2,8,32,128]{3,2,1,0:T(8,128)}, u32[]{:S(2)}) copy-start(f32[2,8,32,128]{3,2,1,0:T(8,128)} %copy-done.3) | copy-start | bytes 786436
  77.5 56.7 %copy-start.2 = (bf16[256,128]{1,0:T(8,128)(2,1)S(1)}, bf16[256,128]{1,0:T(8,128)(2,1)}, u32[]{:S(2)}) copy-start(bf16[256,128]{1,0:T(8,128)(2,1)} %uo_ref.3) | copy-start | bytes 196612
  77.5 56.7 %copy-start.5 = (f32[32,16]{0,1:T(8,128)S(1)}, f32[32,16]{0,1:T(8,128)}, u32[]{:S(2)}) copy-start(f32[32,16]{0,1:T(8,128)} %param.15) | copy-start | bytes 6148
  77.5 56.7 %all-to-all-start.1 = ((f32[128,32,128]{2,1,0:T(8,128)}), f32[128,32,128]{2,1,0:T(8,128)S(1)}, u32[]{:S(2)}, u32[]{:S(2)}) async-start(f32[128,32,128]{2,1,0:T(8,128)} %bitcast.17), calls=%async_computation.1 | async-start | bytes 4194304 | tf_op jit(solution)/shard_map/all_to_all | solution.py:354
  87.2 26.6 %collective-permute-start.8 = (f32[8,32,128]{2,1,0:T(8,128)S(1)}, f32[8,32,128]{2,1,0:T(8,128)S(1)}, u32[]{:S(2)}, u32[]{:S(2)}) collective-permute-start(f32[8,32,128]{2,1,0:T(8,128)S(1)} %get-tuple-element.33), channel_id=1, source_target_pairs={{0,8},{8,0},{16,24},{24,16},{32,40},{40,32},{48,56},{56,48},{64,72... | collective-permute-start | bytes 393224 | tf_op jit(solution)/shard_map/ppermute | solution.py:137
  113.8 11.8 %collective-permute-start.15 = (f32[2,32,128]{2,1,0:T(8,128)S(1)}, f32[2,32,128]{2,1,0:T(8,128)S(1)}, u32[]{:S(2)}, u32[]{:S(2)}) collective-permute-start(f32[2,32,128]{2,1,0:T(8,128)S(1)} %get-tuple-element.25), channel_id=1, source_target_pairs={{0,112},{8,120},{16,96},{24,104},{32,16},{40,24},{48,0},{56,8},{64... | collective-permute-start | bytes 98312 | tf_op jit(solution)/shard_map/ppermute | solution.py:142
  119.1 6.8 %collective-permute-start.9 = (f32[2,32,128]{2,1,0:T(8,128)S(1)}, f32[2,32,128]{2,1,0:T(8,128)S(1)}, u32[]{:S(2)}, u32[]{:S(2)}) collective-permute-start(f32[2,32,128]{2,1,0:T(8,128)S(1)} %get-tuple-element.27), channel_id=1, source_target_pairs={{0,16},{8,24},{16,0},{24,8},{32,48},{40,56},{48,32},{56,40},{64,80... | collective-permute-start | bytes 98312 | tf_op jit(solution)/shard_map/ppermute | solution.py:142
  119.7 8.1 %collective-permute-start.10 = (f32[2,32,128]{2,1,0:T(8,128)S(1)}, f32[2,32,128]{2,1,0:T(8,128)S(1)}, u32[]{:S(2)}, u32[]{:S(2)}) collective-permute-start(f32[2,32,128]{2,1,0:T(8,128)S(1)} %get-tuple-element.28), channel_id=1, source_target_pairs={{0,32},{8,40},{16,48},{24,56},{32,64},{40,72},{48,80},{56,88},{64,... | collective-permute-start | bytes 98312 | tf_op jit(solution)/shard_map/ppermute | solution.py:142
  119.7 8.1 %collective-permute-start.11 = (f32[2,32,128]{2,1,0:T(8,128)S(1)}, f32[2,32,128]{2,1,0:T(8,128)S(1)}, u32[]{:S(2)}, u32[]{:S(2)}) collective-permute-start(f32[2,32,128]{2,1,0:T(8,128)S(1)} %get-tuple-element.29), channel_id=1, source_target_pairs={{0,48},{8,56},{16,32},{24,40},{32,80},{40,88},{48,64},{56,72},{64,... | collective-permute-start | bytes 98312 | tf_op jit(solution)/shard_map/ppermute | solution.py:142
  121.5 6.2 %collective-permute-start.12 = (f32[2,32,128]{2,1,0:T(8,128)S(1)}, f32[2,32,128]{2,1,0:T(8,128)S(1)}, u32[]{:S(2)}, u32[]{:S(2)}) collective-permute-start(f32[2,32,128]{2,1,0:T(8,128)S(1)} %get-tuple-element.30), channel_id=1, source_target_pairs={{0,64},{8,72},{16,80},{24,88},{32,96},{40,104},{48,112},{56,120},{... | collective-permute-start | bytes 98312 | tf_op jit(solution)/shard_map/ppermute | solution.py:142
  125.7 6.7 %collective-permute-start.13 = (f32[2,32,128]{2,1,0:T(8,128)S(1)}, f32[2,32,128]{2,1,0:T(8,128)S(1)}, u32[]{:S(2)}, u32[]{:S(2)}) collective-permute-start(f32[2,32,128]{2,1,0:T(8,128)S(1)} %get-tuple-element.31), channel_id=1, source_target_pairs={{0,80},{8,88},{16,64},{24,72},{32,112},{40,120},{48,96},{56,104},{... | collective-permute-start | bytes 98312 | tf_op jit(solution)/shard_map/ppermute | solution.py:142
  126.0 6.4 %collective-permute-start.14 = (f32[2,32,128]{2,1,0:T(8,128)S(1)}, f32[2,32,128]{2,1,0:T(8,128)S(1)}, u32[]{:S(2)}, u32[]{:S(2)}) collective-permute-start(f32[2,32,128]{2,1,0:T(8,128)S(1)} %get-tuple-element.32), channel_id=1, source_target_pairs={{0,96},{8,104},{16,112},{24,120},{32,0},{40,8},{48,16},{56,24},{64... | collective-permute-start | bytes 98312 | tf_op jit(solution)/shard_map/ppermute | solution.py:142

commit v4 on v3

--- a/solution.py
+++ b/solution.py
@@ -72,28 +72,28 @@
 
     kb = kb_ref[...]
     uo = uo_ref[...]
-    for p in range(2):
+    for n, p in [(n, p) for n in range(2) for p in range(2)]:
         tiles = []
         for a in range(4):
-            both = dot(kb, g_ref[:, p, a].reshape(256, 256))
+            both = dot(kb, g_ref[n * 8 : n * 8 + 8, p, a].reshape(256, 256))
             hi, lo = split(both[0:128] + both[128:256])
             nar = (dot(hi, uo) + dot(lo, uo)).reshape(8, 2, 8, 128)
             tiles += [nar[:, 0].reshape(64, 128), nar[:, 1].reshape(64, 128)]
         tiles = swap_groups(tiles)
         for j in range(8):
-            z_ref[p * 8 + j] = tiles[j].reshape(8, 8, 128)
+            z_ref[p * 8 + j, :, n * 8 : n * 8 + 8, :] = tiles[j].reshape(8, 8, 128)
 
 
 def head(gradient, u_out, ub_t):
     return pl.pallas_call(
         head_kernel,
-        grid=(4,),
+        grid=(2,),
         in_specs=[
-            pl.BlockSpec((8, 2, 4, 32, 256), lambda g: (g, 0, 0, 0, 0)),
+            pl.BlockSpec((16, 2, 4, 32, 256), lambda g: (g, 0, 0, 0, 0)),
             pl.BlockSpec((256, 128), lambda g: (0, 0)),
             pl.BlockSpec((16, 32), lambda g: (0, 0)),
         ],
-        out_specs=pl.BlockSpec((16, 8, 8, 128), lambda g: (0, 0, g, 0)),
+        out_specs=pl.BlockSpec((16, 8, 16, 128), lambda g: (0, 0, g, 0)),
         out_shape=jax.ShapeDtypeStruct((16, 8, 32, 128), F32),
         scratch_shapes=[pltpu.VMEM((256, 256), BF16)],
         compiler_params=pltpu.CompilerParams(vmem_limit_bytes=54 * 1024 * 1024),
@@ -149,7 +149,9 @@
     return new_first, new_second
 
 
-def prep_kernel(uat_ref, ka_hbm, kat_hbm, ka_ref, kat_ref, sems):
+def prep_kernel(uat_ref, ubt_ref, ka_hbm, kat_hbm, kb_hbm, ka_ref, kat_ref, kb_ref, sems):
+    hi, lo = spread_b(ubt_ref[...])
+    kb_ref[...] = jnp.concatenate([hi.T, hi.T, lo.T], axis=1)
     tall = one_hot((1024, 32), lambda r: r // 32, lambda c: c).astype(BF16)
     wide = one_hot((16, 512), lambda r: r, lambda c: c // 32).astype(BF16)
     same = one_hot((1024, 512), lambda r: r % 32, lambda c: c % 32)
@@ -165,6 +167,7 @@
     copies = [
         pltpu.make_async_copy(ka_ref, ka_hbm, sems.at[0]),
         pltpu.make_async_copy(kat_ref, kat_hbm, sems.at[1]),
+        pltpu.make_async_copy(kb_ref, kb_hbm, sems.at[2]),
     ]
     for copy in copies:
         copy.start()
@@ -172,23 +175,25 @@
         copy.wait()
 
 
-def prep(u_at):
+def prep(u_at, ub_t):
     return pl.pallas_call(
         prep_kernel,
         out_shape=(
             jax.ShapeDtypeStruct((2, 1024, 512), BF16),
             jax.ShapeDtypeStruct((2, 512, 1024), BF16),
+            jax.ShapeDtypeStruct((256, 384), BF16),
         ),
-        in_specs=[VMEM],
-        out_specs=(HBM, HBM),
+        in_specs=[VMEM] * 2,
+        out_specs=(HBM,) * 3,
         scratch_shapes=[
             pltpu.VMEM((2, 1024, 512), BF16),
             pltpu.VMEM((2, 512, 1024), BF16),
-            pltpu.SemaphoreType.DMA((2,)),
+            pltpu.VMEM((256, 384), BF16),
+            pltpu.SemaphoreType.DMA((3,)),
         ],
         compiler_params=pltpu.CompilerParams(vmem_limit_bytes=56 * 1024 * 1024),
         name="prep",
-    )(u_at)
+    )(u_at, ub_t)
 
 
 def collect_kernel(*refs):
@@ -299,16 +304,12 @@
     )(fm, sm, *core)
 
 
-def tail_kernel(v_ref, w_ref, uo_ref, ubt_ref, o_ref, kb_ref):
-    @pl.when(pl.program_id(0) == 0)
-    def _():
-        hi, lo = spread_b(ubt_ref[...])
-        kb_ref[...] = jnp.concatenate([hi.T, hi.T, lo.T], axis=1)
-
+def tail_kernel(v_ref, w_ref, uo_ref, kb_ref, o_ref):
     kb = kb_ref[...]
     uo = uo_ref[...]
-    rows = pl.ds(pl.program_id(0) * 8, 8)
-    for p in range(2):
+    for k, p in [(k, p) for k in range(2) for p in range(2)]:
+        rows = pl.ds(pl.program_id(0) * 16 + k * 8, 8)
+        mine = slice(k * 8, k * 8 + 8)
         tiles = swap_groups([v_ref[p * 8 + j, :, rows, :].reshape(64, 128) for j in range(8)])
         for pair in range(2):
             wide = []
@@ -320,25 +321,24 @@
             for n in range(2):
                 a = 2 * pair + n
                 update = dot(expanded[:, n * 128 : n * 128 + 128], uo, ((1,), (1,))).reshape(8, 32, 256)
-                o_ref[:, p, a] = (w_ref[:, p, a].astype(F32) - step_rate * update).astype(BF16)
-
-
-def tail(v, weight, u_out, ub_t):
+                o_ref[mine, p, a] = (w_ref[mine, p, a].astype(F32) - step_rate * update).astype(BF16)
+
+
+def tail(v, weight, u_out, kb):
     return pl.pallas_call(
         tail_kernel,
-        grid=(4,),
+        grid=(2,),
         in_specs=[
             VMEM,
-            pl.BlockSpec((8, 2, 4, 32, 256), lambda g: (g, 0, 0, 0, 0)),
+            pl.BlockSpec((16, 2, 4, 32, 256), lambda g: (g, 0, 0, 0, 0)),
             pl.BlockSpec((256, 128), lambda g: (0, 0)),
-            pl.BlockSpec((16, 32), lambda g: (0, 0)),
+            pl.BlockSpec((256, 384), lambda g: (0, 0)),
         ],
-        out_specs=pl.BlockSpec((8, 2, 4, 32, 256), lambda g: (g, 0, 0, 0, 0)),
+        out_specs=pl.BlockSpec((16, 2, 4, 32, 256), lambda g: (g, 0, 0, 0, 0)),
         out_shape=jax.ShapeDtypeStruct((32, 2, 4, 32, 256), BF16),
-        scratch_shapes=[pltpu.VMEM((256, 384), BF16)],
         compiler_params=pltpu.CompilerParams(vmem_limit_bytes=48 * 1024 * 1024),
         name="tail",
-    )(v, weight, u_out, ub_t)
+    )(v, weight, u_out, kb)
 
 
 def shards(weight, gradient, first_moment, second_moment, u_in, u_out, u_modes_a, u_modes_b):
@@ -349,12 +349,12 @@
     sent = head(gradient, u_out, ub_t).reshape(128, 32, 128)
     got = lax.all_to_all(sent, both, 0, 0, tiled=True).reshape(16, 8, 32, 128)
     packed = collect(pair_exchange(pack(fm, sm, u_in, sent)))
-    ka, kat = prep(u_modes_a.T)
+    ka, kat, kb = prep(u_modes_a.T, ub_t)
     wide, core = mid(got, packed, ka, kat, sent.reshape(got.shape))
     wide = lax.all_to_all(wide.reshape(128, 32, 128), both, 0, 0, tiled=True)
     core = pair_exchange(core)
     new_first, new_second = moments(core, fm, sm)
-    new_weight = tail(wide.reshape(16, 8, 32, 128), weight, u_out, ub_t)
+    new_weight = tail(wide.reshape(16, 8, 32, 128), weight, u_out, kb)
     return new_weight, new_first.reshape(first_moment.shape), new_second.reshape(second_moment.shape)
 
 

time: 144 us -> 142 us (0.986)
  Pallas kernels: 27.8 us -> 25.7 us
    pallas_call x2, Pallas kernels: 15.1 us -> 12.7 us  [the longest x1 6.42 us: head(): pl.pallas_call(head_kernel, grid=(2,), in_specs=[pl.BlockSpec((16, 2, 4,...]
where the time goes in v4:
time: 142 us; the launch traced here: 140 us
  waiting for transfers between devices  60.3 us (42%)
  starting transfers between devices  51.8 us (36%)
  Pallas kernels  25.7 us (18%)
    ppermute x2, waiting for transfers between devices, pair_exchange(): across = lax.ppermute(blocks[1], 'chan', [(c, c ^ 1) for c in range(16)])  54.4 us
    ppermute x14, starting transfers between devices, pair_exchange(): got.append(lax.ppermute(both[f], 'chan', ring))  27.8 us
    all_to_all x1, starting transfers between devices, shards(): got = lax.all_to_all(sent, both, 0, 0, tiled=True).reshape(16, 8, 32, 128)  11.5 us
    all_to_all x1, starting transfers between devices, shards(): wide = lax.all_to_all(wide.reshape(128, 32, 128), both, 0, 0, tiled=True)  9.68 us
    pallas_call x1, Pallas kernels, head(): pl.pallas_call(head_kernel, grid=(2,), in_specs=[pl.BlockSpec((16, 2, 4,...  6.42 us
    pallas_call x1, Pallas kernels, tail(): pl.pallas_call(tail_kernel, grid=(2,), in_specs=[VMEM, pl.BlockSpec((16,...  6.31 us
    ppermute x14, waiting for transfers between devices, pair_exchange(): got.append(lax.ppermute(both[f], 'chan', ring))  5.89 us
    pallas_call x1, Pallas kernels, mid(): pl.pallas_call(mid_kernel, out_shape=(jax.ShapeDtypeStruct((16, 8, 32, 12...  5.58 us
  transfers between devices with their start and end apart: 18, of which 4 were waited for; matrix products, arithmetic and copies ran while one was open for 0% of the time, Pallas kernels for 5%

profile of v4, /device:TPU:1, one launch (start us, length us, event | category | flops | bytes accessed | tf_op | source)
XLA Modules:
  0.0 139.5 jit_solution(10394173578404185834)
XLA Ops:
  0.6 6.4 %head.1.old_hbm = f32[16,8,32,128]{3,2,1,0:T(8,128)} custom-call(bf16[32,2,4,32,256]{4,3,2,1,0:T(8,128)(2,1)} %g_ref.1, bf16[256,128]{1,0:T(8,128)(2,1)} %uo_ref.3, f32[16,32]{1,0:T(8,128)} %bitcast.60), custom_call_target="tpu_custom_call" | custom-call | tf_op jit(solution)/shard_map/head/pallas_call | solution.py:88
  7.1 11.5 %all-to-all-start = ((f32[128,32,128]{2,1,0:T(8,128)}), f32[128,32,128]{2,1,0:T(8,128)S(1)}, u32[]{:S(2)}, u32[]{:S(2)}) async-start(f32[128,32,128]{2,1,0:T(8,128)} %bitcast.1.after_ref), calls=%async_computation | async-start | bytes 4194304 | tf_op jit(solution)/shard_map/all_to_all | solution.py:350
  18.6 1.5 %pack.1 = f32[2,8,96,128]{3,2,1,0:T(8,128)S(1)} custom-call(f32[8,2,32,128]{3,2,1,0:T(8,128)S(1)} %bitcast.54, f32[8,2,32,128]{3,2,1,0:T(8,128)S(1)} %bitcast.56, f32[32,128]{1,0:T(8,128)S(1)} %copy-done.6, f32[128,32,128]{2,1,0:T(8,128)} %bitcast.1.after_ref), custom_call_target="tpu_custom_call" | custom-call | tf_op jit(solution)/shard_map/pack/pallas_call | solution.py:121
  20.0 0.1 slice_bitcast_fusion
  20.1 1.4 %collective-permute-start = (f32[8,96,128]{2,1,0:T(8,128)S(1)}, f32[8,96,128]{2,1,0:T(8,128)S(1)}, u32[]{:S(2)}, u32[]{:S(2)}) collective-permute-start(f32[8,96,128]{2,1,0:T(8,128)S(1)} %get-tuple-element.25), channel_id=1, source_target_pairs={{0,8},{8,0},{16,24},{24,16},{32,40},{40,32},{48,56},{56,48},{64,72... | collective-permute-start | bytes 1179656 | tf_op jit(solution)/shard_map/ppermute | solution.py:137
  21.5 29.3 %collective-permute-done = f32[8,96,128]{2,1,0:T(8,128)S(1)} collective-permute-done((f32[8,96,128]{2,1,0:T(8,128)S(1)}, f32[8,96,128]{2,1,0:T(8,128)S(1)}, u32[]{:S(2)}, u32[]{:S(2)}) %collective-permute-start) | collective-permute-done | bytes 393248 | tf_op jit(solution)/shard_map/ppermute | solution.py:137
  50.8 0.1 fusion.14
  50.9 5.3 %collective-permute-start.7 = (f32[2,96,128]{2,1,0:T(8,128)S(1)}, f32[2,96,128]{2,1,0:T(8,128)S(1)}, u32[]{:S(2)}, u32[]{:S(2)}) collective-permute-start(f32[2,96,128]{2,1,0:T(8,128)S(1)} %get-tuple-element.17), channel_id=1, source_target_pairs={{0,112},{8,120},{16,96},{24,104},{32,16},{40,24},{48,0},{56,8},{64... | collective-permute-start | bytes 294920 | tf_op jit(solution)/shard_map/ppermute | solution.py:142
  56.2 0.5 collective-permute-start.1
  56.7 0.0 collective-permute-start.2
  56.7 1.9 %collective-permute-start.3 = (f32[2,96,128]{2,1,0:T(8,128)S(1)}, f32[2,96,128]{2,1,0:T(8,128)S(1)}, u32[]{:S(2)}, u32[]{:S(2)}) collective-permute-start(f32[2,96,128]{2,1,0:T(8,128)S(1)} %get-tuple-element.21), channel_id=1, source_target_pairs={{0,48},{8,56},{16,32},{24,40},{32,80},{40,88},{48,64},{56,72},{64,... | collective-permute-start | bytes 294920 | tf_op jit(solution)/shard_map/ppermute | solution.py:142
  58.6 4.1 %collective-permute-start.4 = (f32[2,96,128]{2,1,0:T(8,128)S(1)}, f32[2,96,128]{2,1,0:T(8,128)S(1)}, u32[]{:S(2)}, u32[]{:S(2)}) collective-permute-start(f32[2,96,128]{2,1,0:T(8,128)S(1)} %get-tuple-element.22), channel_id=1, source_target_pairs={{0,64},{8,72},{16,80},{24,88},{32,96},{40,104},{48,112},{56,120},{... | collective-permute-start | bytes 294920 | tf_op jit(solution)/shard_map/ppermute | solution.py:142
  62.7 0.3 collective-permute-start.5
  63.0 1.8 %collective-permute-start.6 = (f32[2,96,128]{2,1,0:T(8,128)S(1)}, f32[2,96,128]{2,1,0:T(8,128)S(1)}, u32[]{:S(2)}, u32[]{:S(2)}) collective-permute-start(f32[2,96,128]{2,1,0:T(8,128)S(1)} %get-tuple-element.24), channel_id=1, source_target_pairs={{0,96},{8,104},{16,112},{24,120},{32,0},{40,8},{48,16},{56,24},{64... | collective-permute-start | bytes 294920 | tf_op jit(solution)/shard_map/ppermute | solution.py:142
  64.8 4.0 %prep.1 = (bf16[2,1024,512]{2,1,0:T(8,128)(2,1)}, bf16[2,512,1024]{2,1,0:T(8,128)(2,1)}, bf16[256,384]{1,0:T(8,128)(2,1)}) custom-call(f32[16,32]{1,0:T(8,128)} %bitcast.62, f32[16,32]{1,0:T(8,128)} %bitcast.61), custom_call_target="tpu_custom_call" | custom-call | tf_op jit(solution)/shard_map/prep/pallas_call | solution.py:179
  68.8 1.3 collective-permute-done.5.refs_5_
  70.1 0.1 collect.1.pk_ref
  70.2 5.6 %mid.1 = (f32[16,8,32,128]{3,2,1,0:T(8,128)}, f32[2,8,32,128]{3,2,1,0:T(8,128)S(1)}) custom-call(f32[16,8,32,128]{3,2,1,0:T(8,128)S(1)} %bitcast.52, bf16[2,1024,512]{2,1,0:T(8,128)(2,1)} %get-tuple-element.10.ka_hbm, bf16[2,512,1024]{2,1,0:T(8,128)(2,1)} %get-tuple-element.11.kat_hbm, ...), custom_call_target="tpu_custom_call", output_to_operand_aliasing={{0}: (3, {})} | custom-call | tf_op jit(solution)/shard_map/mid/pallas_call | solution.py:261
  75.7 0.0 copy-start.3
  75.8 0.7 copy-done.3
  76.5 9.7 %all-to-all-start.1 = ((f32[128,32,128]{2,1,0:T(8,128)}), f32[128,32,128]{2,1,0:T(8,128)S(1)}, u32[]{:S(2)}, u32[]{:S(2)}) async-start(f32[128,32,128]{2,1,0:T(8,128)} %bitcast.17), calls=%async_computation.1 | async-start | bytes 4194304 | tf_op jit(solution)/shard_map/all_to_all | solution.py:354
  86.2 1.4 %collective-permute-start.8 = (f32[8,32,128]{2,1,0:T(8,128)S(1)}, f32[8,32,128]{2,1,0:T(8,128)S(1)}, u32[]{:S(2)}, u32[]{:S(2)}) collective-permute-start(f32[8,32,128]{2,1,0:T(8,128)S(1)} %get-tuple-element.35), channel_id=1, source_target_pairs={{0,8},{8,0},{16,24},{24,16},{32,40},{40,32},{48,56},{56,48},{64,72... | collective-permute-start | bytes 393224 | tf_op jit(solution)/shard_map/ppermute | solution.py:137
  87.6 25.2 %collective-permute-done.8 = f32[8,32,128]{2,1,0:T(8,128)S(1)} collective-permute-done((f32[8,32,128]{2,1,0:T(8,128)S(1)}, f32[8,32,128]{2,1,0:T(8,128)S(1)}, u32[]{:S(2)}, u32[]{:S(2)}) %collective-permute-start.8) | collective-permute-done | bytes 131104 | tf_op jit(solution)/shard_map/ppermute | solution.py:137
  112.8 5.3 %collective-permute-start.15 = (f32[2,32,128]{2,1,0:T(8,128)S(1)}, f32[2,32,128]{2,1,0:T(8,128)S(1)}, u32[]{:S(2)}, u32[]{:S(2)}) collective-permute-start(f32[2,32,128]{2,1,0:T(8,128)S(1)} %get-tuple-element.27), channel_id=1, source_target_pairs={{0,112},{8,120},{16,96},{24,104},{32,16},{40,24},{48,0},{56,8},{64... | collective-permute-start | bytes 98312 | tf_op jit(solution)/shard_map/ppermute | solution.py:142
  118.1 0.5 collective-permute-start.9
  118.6 1.9 %collective-permute-start.11 = (f32[2,32,128]{2,1,0:T(8,128)S(1)}, f32[2,32,128]{2,1,0:T(8,128)S(1)}, u32[]{:S(2)}, u32[]{:S(2)}) collective-permute-start(f32[2,32,128]{2,1,0:T(8,128)S(1)} %get-tuple-element.31), channel_id=1, source_target_pairs={{0,48},{8,56},{16,32},{24,40},{32,80},{40,88},{48,64},{56,72},{64,... | collective-permute-start | bytes 98312 | tf_op jit(solution)/shard_map/ppermute | solution.py:142
  120.5 4.1 %collective-permute-start.12 = (f32[2,32,128]{2,1,0:T(8,128)S(1)}, f32[2,32,128]{2,1,0:T(8,128)S(1)}, u32[]{:S(2)}, u32[]{:S(2)}) collective-permute-start(f32[2,32,128]{2,1,0:T(8,128)S(1)} %get-tuple-element.32), channel_id=1, source_target_pairs={{0,64},{8,72},{16,80},{24,88},{32,96},{40,104},{48,112},{56,120},{... | collective-permute-start | bytes 98312 | tf_op jit(solution)/shard_map/ppermute | solution.py:142
  124.7 0.3 collective-permute-start.13
  124.9 1.8 %collective-permute-start.14 = (f32[2,32,128]{2,1,0:T(8,128)S(1)}, f32[2,32,128]{2,1,0:T(8,128)S(1)}, u32[]{:S(2)}, u32[]{:S(2)}) collective-permute-start(f32[2,32,128]{2,1,0:T(8,128)S(1)} %get-tuple-element.34), channel_id=1, source_target_pairs={{0,96},{8,104},{16,112},{24,120},{32,0},{40,8},{48,16},{56,24},{64... | collective-permute-start | bytes 98312 | tf_op jit(solution)/shard_map/ppermute | solution.py:142
  126.7 4.6 %collective-permute-done.13.refs_5_ = f32[2,32,128]{2,1,0:T(8,128)S(1)} collective-permute-done((f32[2,32,128]{2,1,0:T(8,128)S(1)}, f32[2,32,128]{2,1,0:T(8,128)S(1)}, u32[]{:S(2)}, u32[]{:S(2)}) %collective-permute-start.13) | collective-permute-done | bytes 32800 | tf_op jit(solution)/shard_map/ppermute | solution.py:142
  131.3 1.9 %moments.1 = (f32[8,2,32,128]{3,2,1,0:T(8,128)}, f32[8,2,32,128]{3,2,1,0:T(8,128)}) custom-call(f32[8,2,32,128]{3,2,1,0:T(8,128)S(1)} %bitcast.55, f32[8,2,32,128]{3,2,1,0:T(8,128)S(1)} %bitcast.57, f32[2,32,128]{2,1,0:T(8,128)S(1)} %get-tuple-element.28.refs_0_, f32[2,32,128]{2,1,0:T(8,128)S(1)} %collective-permute-done.9.refs_1_, ...), custom_call_target="tpu_custom_call" | custom-call | tf_op jit(solution)/shard_map/moments/pallas_call | solution.py:298
  133.2 6.3 %tail.1 = bf16[32,2,4,32,256]{4,3,2,1,0:T(8,128)(2,1)} custom-call(f32[16,8,32,128]{3,2,1,0:T(8,128)S(1)} %bitcast.53, bf16[32,2,4,32,256]{4,3,2,1,0:T(8,128)(2,1)} %w_ref.1, bf16[256,128]{1,0:T(8,128)(2,1)S(1)} %copy-done.2, bf16[256,384]{1,0:T(8,128)(2,1)S(1)} %copy-done.5), custom_call_target="tpu_custom_call" | custom-call | tf_op jit(solution)/shard_map/tail/pallas_call | solution.py:328
  (29 shorter events, 0.1 us)
Async XLA Ops:
  7.0 11.5 %copy-start = (f32[8,2,16,2,128]{4,3,2,1,0:T(2,128)S(1)}, f32[8,2,16,2,128]{4,3,2,1,0:T(2,128)}, u32[]{:S(2)}) copy-start(f32[8,2,16,2,128]{4,3,2,1,0:T(2,128)} %param.10) | copy-start | bytes 786436
  7.1 11.5 %copy-start.1 = (f32[8,2,16,2,128]{4,3,2,1,0:T(2,128)S(1)}, f32[8,2,16,2,128]{4,3,2,1,0:T(2,128)}, u32[]{:S(2)}) copy-start(f32[8,2,16,2,128]{4,3,2,1,0:T(2,128)} %param.11) | copy-start | bytes 786436
  7.1 11.5 %copy-start.6 = (f32[32,128]{1,0:T(8,128)S(1)}, f32[32,128]{1,0:T(8,128)}, u32[]{:S(2)}) copy-start(f32[32,128]{1,0:T(8,128)} %ui_ref.1) | copy-start | bytes 49156
  7.1 63.1 %all-to-all-start = ((f32[128,32,128]{2,1,0:T(8,128)}), f32[128,32,128]{2,1,0:T(8,128)S(1)}, u32[]{:S(2)}, u32[]{:S(2)}) async-start(f32[128,32,128]{2,1,0:T(8,128)} %bitcast.1.after_ref), calls=%async_computation | async-start | bytes 4194304 | tf_op jit(solution)/shard_map/all_to_all | solution.py:350
  20.1 30.7 %collective-permute-start = (f32[8,96,128]{2,1,0:T(8,128)S(1)}, f32[8,96,128]{2,1,0:T(8,128)S(1)}, u32[]{:S(2)}, u32[]{:S(2)}) collective-permute-start(f32[8,96,128]{2,1,0:T(8,128)S(1)} %get-tuple-element.25), channel_id=1, source_target_pairs={{0,8},{8,0},{16,24},{24,16},{32,40},{40,32},{48,56},{56,48},{64,72... | collective-permute-start | bytes 1179656 | tf_op jit(solution)/shard_map/ppermute | solution.py:137
  50.9 11.8 %collective-permute-start.7 = (f32[2,96,128]{2,1,0:T(8,128)S(1)}, f32[2,96,128]{2,1,0:T(8,128)S(1)}, u32[]{:S(2)}, u32[]{:S(2)}) collective-permute-start(f32[2,96,128]{2,1,0:T(8,128)S(1)} %get-tuple-element.17), channel_id=1, source_target_pairs={{0,112},{8,120},{16,96},{24,104},{32,16},{40,24},{48,0},{56,8},{64... | collective-permute-start | bytes 294920 | tf_op jit(solution)/shard_map/ppermute | solution.py:142
  56.2 6.8 %collective-permute-start.1 = (f32[2,96,128]{2,1,0:T(8,128)S(1)}, f32[2,96,128]{2,1,0:T(8,128)S(1)}, u32[]{:S(2)}, u32[]{:S(2)}) collective-permute-start(f32[2,96,128]{2,1,0:T(8,128)S(1)} %get-tuple-element.19), channel_id=1, source_target_pairs={{0,16},{8,24},{16,0},{24,8},{32,48},{40,56},{48,32},{56,40},{64,80... | collective-permute-start | bytes 294920 | tf_op jit(solution)/shard_map/ppermute | solution.py:142
  56.7 12.1 %collective-permute-start.2 = (f32[2,96,128]{2,1,0:T(8,128)S(1)}, f32[2,96,128]{2,1,0:T(8,128)S(1)}, u32[]{:S(2)}, u32[]{:S(2)}) collective-permute-start(f32[2,96,128]{2,1,0:T(8,128)S(1)} %get-tuple-element.20), channel_id=1, source_target_pairs={{0,32},{8,40},{16,48},{24,56},{32,64},{40,72},{48,80},{56,88},{64,... | collective-permute-start | bytes 294920 | tf_op jit(solution)/shard_map/ppermute | solution.py:142
  56.7 12.1 %collective-permute-start.3 = (f32[2,96,128]{2,1,0:T(8,128)S(1)}, f32[2,96,128]{2,1,0:T(8,128)S(1)}, u32[]{:S(2)}, u32[]{:S(2)}) collective-permute-start(f32[2,96,128]{2,1,0:T(8,128)S(1)} %get-tuple-element.21), channel_id=1, source_target_pairs={{0,48},{8,56},{16,32},{24,40},{32,80},{40,88},{48,64},{56,72},{64,... | collective-permute-start | bytes 294920 | tf_op jit(solution)/shard_map/ppermute | solution.py:142
  58.6 10.3 %collective-permute-start.4 = (f32[2,96,128]{2,1,0:T(8,128)S(1)}, f32[2,96,128]{2,1,0:T(8,128)S(1)}, u32[]{:S(2)}, u32[]{:S(2)}) collective-permute-start(f32[2,96,128]{2,1,0:T(8,128)S(1)} %get-tuple-element.22), channel_id=1, source_target_pairs={{0,64},{8,72},{16,80},{24,88},{32,96},{40,104},{48,112},{56,120},{... | collective-permute-start | bytes 294920 | tf_op jit(solution)/shard_map/ppermute | solution.py:142
  62.7 7.4 %collective-permute-start.5 = (f32[2,96,128]{2,1,0:T(8,128)S(1)}, f32[2,96,128]{2,1,0:T(8,128)S(1)}, u32[]{:S(2)}, u32[]{:S(2)}) collective-permute-start(f32[2,96,128]{2,1,0:T(8,128)S(1)} %get-tuple-element.23), channel_id=1, source_target_pairs={{0,80},{8,88},{16,64},{24,72},{32,112},{40,120},{48,96},{56,104},{... | collective-permute-start | bytes 294920 | tf_op jit(solution)/shard_map/ppermute | solution.py:142
  63.0 7.1 %collective-permute-start.6 = (f32[2,96,128]{2,1,0:T(8,128)S(1)}, f32[2,96,128]{2,1,0:T(8,128)S(1)}, u32[]{:S(2)}, u32[]{:S(2)}) collective-permute-start(f32[2,96,128]{2,1,0:T(8,128)S(1)} %get-tuple-element.24), channel_id=1, source_target_pairs={{0,96},{8,104},{16,112},{24,120},{32,0},{40,8},{48,16},{56,24},{64... | collective-permute-start | bytes 294920 | tf_op jit(solution)/shard_map/ppermute | solution.py:142
  75.7 0.7 copy-start.3
  76.5 9.7 %copy-start.4 = (f32[2,8,32,128]{3,2,1,0:T(8,128)S(1)}, f32[2,8,32,128]{3,2,1,0:T(8,128)}, u32[]{:S(2)}) copy-start(f32[2,8,32,128]{3,2,1,0:T(8,128)} %copy-done.3) | copy-start | bytes 786436
  76.5 56.7 %copy-start.2 = (bf16[256,128]{1,0:T(8,128)(2,1)S(1)}, bf16[256,128]{1,0:T(8,128)(2,1)}, u32[]{:S(2)}) copy-start(bf16[256,128]{1,0:T(8,128)(2,1)} %uo_ref.3) | copy-start | bytes 196612
  76.5 56.7 %copy-start.5 = (bf16[256,384]{1,0:T(8,128)(2,1)S(1)}, bf16[256,384]{1,0:T(8,128)(2,1)}, u32[]{:S(2)}) copy-start(bf16[256,384]{1,0:T(8,128)(2,1)} %get-tuple-element.13.kb_ref) | copy-start | bytes 589828
  76.5 56.7 %all-to-all-start.1 = ((f32[128,32,128]{2,1,0:T(8,128)}), f32[128,32,128]{2,1,0:T(8,128)S(1)}, u32[]{:S(2)}, u32[]{:S(2)}) async-start(f32[128,32,128]{2,1,0:T(8,128)} %bitcast.17), calls=%async_computation.1 | async-start | bytes 4194304 | tf_op jit(solution)/shard_map/all_to_all | solution.py:354
  86.2 26.6 %collective-permute-start.8 = (f32[8,32,128]{2,1,0:T(8,128)S(1)}, f32[8,32,128]{2,1,0:T(8,128)S(1)}, u32[]{:S(2)}, u32[]{:S(2)}) collective-permute-start(f32[8,32,128]{2,1,0:T(8,128)S(1)} %get-tuple-element.35), channel_id=1, source_target_pairs={{0,8},{8,0},{16,24},{24,16},{32,40},{40,32},{48,56},{56,48},{64,72... | collective-permute-start | bytes 393224 | tf_op jit(solution)/shard_map/ppermute | solution.py:137
  112.8 11.8 %collective-permute-start.15 = (f32[2,32,128]{2,1,0:T(8,128)S(1)}, f32[2,32,128]{2,1,0:T(8,128)S(1)}, u32[]{:S(2)}, u32[]{:S(2)}) collective-permute-start(f32[2,32,128]{2,1,0:T(8,128)S(1)} %get-tuple-element.27), channel_id=1, source_target_pairs={{0,112},{8,120},{16,96},{24,104},{32,16},{40,24},{48,0},{56,8},{64... | collective-permute-start | bytes 98312 | tf_op jit(solution)/shard_map/ppermute | solution.py:142
  118.1 6.8 %collective-permute-start.9 = (f32[2,32,128]{2,1,0:T(8,128)S(1)}, f32[2,32,128]{2,1,0:T(8,128)S(1)}, u32[]{:S(2)}, u32[]{:S(2)}) collective-permute-start(f32[2,32,128]{2,1,0:T(8,128)S(1)} %get-tuple-element.29), channel_id=1, source_target_pairs={{0,16},{8,24},{16,0},{24,8},{32,48},{40,56},{48,32},{56,40},{64,80... | collective-permute-start | bytes 98312 | tf_op jit(solution)/shard_map/ppermute | solution.py:142
  118.6 8.1 %collective-permute-start.10 = (f32[2,32,128]{2,1,0:T(8,128)S(1)}, f32[2,32,128]{2,1,0:T(8,128)S(1)}, u32[]{:S(2)}, u32[]{:S(2)}) collective-permute-start(f32[2,32,128]{2,1,0:T(8,128)S(1)} %get-tuple-element.30), channel_id=1, source_target_pairs={{0,32},{8,40},{16,48},{24,56},{32,64},{40,72},{48,80},{56,88},{64,... | collective-permute-start | bytes 98312 | tf_op jit(solution)/shard_map/ppermute | solution.py:142
  118.6 8.1 %collective-permute-start.11 = (f32[2,32,128]{2,1,0:T(8,128)S(1)}, f32[2,32,128]{2,1,0:T(8,128)S(1)}, u32[]{:S(2)}, u32[]{:S(2)}) collective-permute-start(f32[2,32,128]{2,1,0:T(8,128)S(1)} %get-tuple-element.31), channel_id=1, source_target_pairs={{0,48},{8,56},{16,32},{24,40},{32,80},{40,88},{48,64},{56,72},{64,... | collective-permute-start | bytes 98312 | tf_op jit(solution)/shard_map/ppermute | solution.py:142
  120.5 6.2 %collective-permute-start.12 = (f32[2,32,128]{2,1,0:T(8,128)S(1)}, f32[2,32,128]{2,1,0:T(8,128)S(1)}, u32[]{:S(2)}, u32[]{:S(2)}) collective-permute-start(f32[2,32,128]{2,1,0:T(8,128)S(1)} %get-tuple-element.32), channel_id=1, source_target_pairs={{0,64},{8,72},{16,80},{24,88},{32,96},{40,104},{48,112},{56,120},{... | collective-permute-start | bytes 98312 | tf_op jit(solution)/shard_map/ppermute | solution.py:142
  124.7 6.7 %collective-permute-start.13 = (f32[2,32,128]{2,1,0:T(8,128)S(1)}, f32[2,32,128]{2,1,0:T(8,128)S(1)}, u32[]{:S(2)}, u32[]{:S(2)}) collective-permute-start(f32[2,32,128]{2,1,0:T(8,128)S(1)} %get-tuple-element.33), channel_id=1, source_target_pairs={{0,80},{8,88},{16,64},{24,72},{32,112},{40,120},{48,96},{56,104},{... | collective-permute-start | bytes 98312 | tf_op jit(solution)/shard_map/ppermute | solution.py:142
  124.9 6.4 %collective-permute-start.14 = (f32[2,32,128]{2,1,0:T(8,128)S(1)}, f32[2,32,128]{2,1,0:T(8,128)S(1)}, u32[]{:S(2)}, u32[]{:S(2)}) collective-permute-start(f32[2,32,128]{2,1,0:T(8,128)S(1)} %get-tuple-element.34), channel_id=1, source_target_pairs={{0,96},{8,104},{16,112},{24,120},{32,0},{40,8},{48,16},{56,24},{64... | collective-permute-start | bytes 98312 | tf_op jit(solution)/shard_map/ppermute | solution.py:142
